TPU v7x, 256 devices: a whole 4x4x8 slice. The times are simulated.
256 devices in a mesh: seq: 32 (over z, y), head: 8 (over x, core).
Axes of the slice: x: 4, y: 4, z: 8, core: 2. Of those that a mesh axis runs over, the one named last changes fastest.
Arguments:
- inputs: bfloat16 [32768, 5120], P('seq', 'head'), may hold values from -0.59765625 to 0.59765625
- gates: bfloat16 [32768, 5120], P('seq', 'head'), may hold values from -6 to 6
- write_keys: bfloat16 [32768, 128], P('seq'), may hold values from -6 to 6
- read_keys: bfloat16 [32768, 128], P('seq'), may hold values from -0.125 to 0.125
- log_decay: float32 [80, 32768], P('head', 'seq'), may hold values from -3 to 0
- skip_gain: float32 [80], P('head'), may hold values from 0.5 to 4
- doc_ids: int32 [32768], P('seq'), may hold values from 0 to 3, never falling along the last dimension, each value on 1 to 16384 neighbouring positions
- out_weight: bfloat16 [5120, 2560], P('head'), may hold values from -0.078125 to 0.078125
- grad_out: bfloat16 [32768, 2560], P(('seq', 'head')), may hold values from -6 to 6
Outputs:
- mixed_out: bfloat16 [32768, 2560], P(('seq', 'head'))
- grad_inputs: bfloat16 [32768, 5120], P('seq', 'head')
Inputs may be any that keep to these rules, and one draw needn't show every extreme that they name: `doc_ids`: document ids never fall along the sequence; every document has 1 to 16384 tokens and one has exactly 16384.
All inputs are finite; a program needn't handle non-finite values.
Results may differ from a plain program's by a relative error of at most 0.02.
Values may be sent and summed in bfloat16 or wider, within the bound.
A program may use at most 128 MiB of HBM per device.

v0:
```python
import jax
import jax.numpy as jnp
from jax import lax
from jax.sharding import Mesh
from jax.sharding import PartitionSpec as P

GROUP = 256
SEQ = ("seq_0", "seq_1")
HEAD = ("head_0", "head_1")
SEQ_HEAD = ("seq_0", "seq_1", "head_0", "head_1")


def passed_along(block, axis, distance):
    devices = range(lax.axis_size(axis))
    route = [(i - distance, i) for i in devices if i - distance in devices]
    return lax.ppermute(block, axis, route)


def joined_along(pieces, dim):
    pieces = jnp.moveaxis(pieces, 0, dim)
    shape = pieces.shape
    return pieces.reshape(*shape[:dim], shape[dim] * shape[dim + 1], *shape[dim + 2 :])


def gather_in_order(shard, axes, sequence):
    pieces = shard[None]
    for k in sequence:
        pieces = lax.all_gather(pieces, axes[k], axis=0, tiled=True)
    current = [lax.axis_size(axes[k]) for k in reversed(sequence)]
    pieces = pieces.reshape(*current, *shard.shape)
    turned = sorted(range(len(sequence)), key=lambda place: sequence[len(sequence) - 1 - place])
    return pieces.transpose(*turned, *range(len(sequence), pieces.ndim)).reshape(-1, *shard.shape)


def whole_of(shard, axes, sequence, dim):
    return joined_along(gather_in_order(shard, axes, sequence), dim)


def nothing_yet(shard, identity):
    return jax.tree.map(
        lambda part, zero: jnp.zeros_like(part) + jnp.asarray(zero, part.dtype), shard, identity
    )


def entering_2(shard, axes, combine, identity, reverse):
    before = start = nothing_yet(shard, identity)
    so_far = shard
    for axis in reversed(axes):
        devices, place = (lax.axis_size(axis), lax.axis_index(axis))
        pieces = jax.tree.map(
            lambda part, kind: lax.all_gather(part.astype(kind), axis),
            so_far,
            (jnp.bfloat16, jnp.bfloat16),
        )
        inside, so_far = (start, start)
        for k in reversed(range(devices)) if reverse else range(devices):
            passed = k > place if reverse else k < place
            so_far = combine(
                so_far, jax.tree.map(lambda part, own: part[k].astype(own.dtype), pieces, shard)
            )
            inside = jax.tree.map(lambda new, old: jnp.where(passed, new, old), so_far, inside)
        before = combine(inside, before)
    return before


def group_terms(write_blk, read_blk, decay_blk, doc_blk, before):
    block_len = doc_blk.shape[0]
    cumul = jnp.cumsum(decay_blk, axis=1)
    positions = jnp.arange(block_len)
    causal_same = (doc_blk[:, None] == doc_blk[None, :]) & (
        positions[:, None] >= positions[None, :]
    )
    spread = jnp.where(causal_same[None], cumul[:, :, None] - cumul[:, None, :], 0.0)
    decay_matrix = jnp.where(causal_same[None], jnp.exp(spread), 0.0)
    scores = jnp.dot(read_blk, write_blk.T, preferred_element_type=jnp.float32)
    weights = (decay_matrix * scores[None]).astype(jnp.bfloat16)
    entry_w = jnp.where((doc_blk == before)[None], jnp.exp(cumul), 0.0)
    exit_w = jnp.where(
        (doc_blk == doc_blk[block_len - 1])[None], jnp.exp(cumul[:, block_len - 1 :] - cumul), 0.0
    )
    return (weights, entry_w, exit_w, entry_w[:, block_len - 1])


def combine(earlier, later):
    return (earlier[0] * later[0], later[0][:, None, None] * earlier[1] + later[1])


def shards(
    inputs, gates, write_keys, read_keys, log_decay, skip_gain, doc_ids, out_weight, grad_out
):
    tok_rows, inner = inputs.shape
    head_count = log_decay.shape[0]
    head_width = inner // head_count
    state_width = write_keys.shape[1]
    group_count = tok_rows // GROUP
    before = passed_along(doc_ids[tok_rows - 1 :] + 1, SEQ, 1) - 1
    doc_blocks = doc_ids.reshape(group_count, GROUP)
    befores = jnp.concatenate([before, doc_blocks[:-1, GROUP - 1]])
    blocks_b = write_keys.reshape(group_count, GROUP, state_width)
    blocks_c = read_keys.reshape(group_count, GROUP, state_width)
    blocks_d = log_decay.reshape(head_count, group_count, GROUP).transpose(1, 0, 2)
    blocks_x = inputs.reshape(group_count, GROUP, head_count, head_width)
    weights, entry_w, exit_w, decays = jax.vmap(group_terms)(
        blocks_b, blocks_c, blocks_d, doc_blocks, befores
    )
    entry_t = jnp.swapaxes(entry_w, 1, 2)[..., None]
    exit_t = jnp.swapaxes(exit_w, 1, 2)[..., None]
    skip_full = skip_gain[:, None]
    inner_mixed = jnp.einsum(
        "khts,kshp->kthp", weights, blocks_x, preferred_element_type=jnp.float32
    )
    write_scaled = (exit_t * blocks_x.astype(jnp.float32)).astype(jnp.bfloat16)
    own_states = jnp.einsum(
        "kshp,ksn->khpn", write_scaled, blocks_b, preferred_element_type=jnp.float32
    )
    empty_state = jnp.zeros((head_count, head_width, state_width), jnp.float32)
    unit_decay = jnp.ones((head_count,), jnp.float32)
    running = empty_state
    run_decay = unit_decay
    enter_states = []
    enter_decays = []
    for position in range(group_count):
        enter_states.append(running)
        enter_decays.append(run_decay)
        running = decays[position][:, None, None] * running + own_states[position]
        run_decay = decays[position] * run_decay
    silu_gate = jax.nn.silu(gates.astype(jnp.float32))
    grad_gated = lax.dot_general(
        whole_of(grad_out, HEAD, (0, 1), 0),
        out_weight,
        (((1,), (1,)), ((), ())),
        preferred_element_type=jnp.float32,
    )
    grad_mix = (grad_gated * silu_gate).astype(jnp.bfloat16)
    blocks_dy = grad_mix.reshape(group_count, GROUP, head_count, head_width)
    inner_grad = jnp.einsum(
        "khts,kthp->kshp", weights, blocks_dy, preferred_element_type=jnp.float32
    )
    grad_scaled = (entry_t * blocks_dy.astype(jnp.float32)).astype(jnp.bfloat16)
    grad_states = jnp.einsum(
        "kthp,ktn->khpn", grad_scaled, blocks_c, preferred_element_type=jnp.float32
    )
    running_back = empty_state
    back_decay = unit_decay
    exit_states = []
    exit_decays = []
    for position in reversed(range(group_count)):
        exit_states.insert(0, running_back)
        exit_decays.insert(0, back_decay)
        running_back = grad_states[position] + decays[position][:, None, None] * running_back
        back_decay = decays[position] * back_decay
    state_in = entering_2((run_decay, running), SEQ, combine, (unit_decay, empty_state), False)[1]
    grad_in = entering_2((run_decay, running_back), SEQ, combine, (unit_decay, empty_state), True)[
        1
    ]
    entering = jnp.stack(
        [
            enter_states[position] + enter_decays[position][:, None, None] * state_in
            for position in range(group_count)
        ]
    ).astype(jnp.bfloat16)
    carried = (
        jnp.einsum("ktn,khpn->kthp", blocks_c, entering, preferred_element_type=jnp.float32)
        * entry_t
    )
    mixed = inner_mixed + carried + skip_full * blocks_x.astype(jnp.float32)
    gated = (mixed.reshape(tok_rows, inner) * silu_gate).astype(jnp.bfloat16)
    mixed_out = lax.psum_scatter(
        jnp.dot(gated, out_weight, preferred_element_type=jnp.float32).astype(jnp.bfloat16),
        HEAD,
        scatter_dimension=0,
        tiled=True,
    )
    arriving = jnp.stack(
        [
            exit_states[position] + exit_decays[position][:, None, None] * grad_in
            for position in range(group_count)
        ]
    ).astype(jnp.bfloat16)
    carried_grad = (
        jnp.einsum("ksn,khpn->kshp", blocks_b, arriving, preferred_element_type=jnp.float32)
        * exit_t
    )
    grad_inputs = (inner_grad + carried_grad + skip_full * blocks_dy.astype(jnp.float32)).astype(
        jnp.bfloat16
    )
    return (mixed_out, grad_inputs.reshape(tok_rows, inner))


def solution(mesh):
    split = Mesh(mesh.devices.reshape(8, 4, 4, 2), ("seq_0", "seq_1", "head_0", "head_1"))
    return jax.shard_map(
        shards,
        mesh=split,
        in_specs=(
            P(SEQ, HEAD),
            P(SEQ, HEAD),
            P(SEQ, None),
            P(SEQ, None),
            P(HEAD, SEQ),
            P(HEAD),
            P(SEQ),
            P(HEAD, None),
            P(SEQ_HEAD, None),
        ),
        out_specs=(P(SEQ_HEAD, None), P(SEQ, HEAD)),
        check_vma=False,
    )
```

profile of v0, /device:TPU:1, one launch (start us, length us, event | category | flops | bytes accessed | tf_op | source)
XLA Modules:
  0.0 245.2 jit_solution(7034171664779118965)
XLA Ops:
  7.2 0.7 all-gather.15.cloned.1.call-update
  8.0 1.5 slice.212
  10.1 4.7 %collective-permute-start = (s32[1]{0:T(128)}, s32[1]{0:T(128)}, u32[]{:S(2)}, u32[]{:S(2)}) collective-permute-start(s32[1]{0:T(128)} %add.280), channel_id=1, source_target_pairs={{0,8},{8,16},{16,24},{24,32},{32,40},{40,48},{48,56},{56,64},{64,7... | collective-permute-start | bytes 20 | tf_op jit(solution)/shard_map/ppermute | solution.py:16
  14.8 0.7 eq.45
  15.5 0.9 reshape.396
  16.4 2.3 reduce-window.6
  19.8 2.5 %copy.66 = bf16[1024,640]{0,1:T(8,128)(2,1)} copy(bf16[1024,640]{1,0:T(8,128)(2,1)} %param.9) | data formatting | bytes 2621440 | tf_op args[0]
  23.5 1.5 exponential_select_fusion
  25.8 3.8 %reshape.401 = bf16[4,256,10,64]{1,0,3,2:T(4,128)(2,1)} reshape(bf16[1024,640]{0,1:T(8,128)(2,1)} %copy.66) | data formatting | bytes 2621440 | tf_op jit(solution)/shard_map/reshape | solution.py:102
  29.6 8.7 %all-gather = bf16[4,10,1]{1,2,0:T(2,128)(2,1)S(1)} all-gather(bf16[1,10,1]{1,2,0:T(2,128)(2,1)S(1)} %copy.68), channel_id=2, replica_groups=mesh['seq_0'=8,'seq_1'=4,'head_0'=4,'head_1'=2] {'seq_1'}, dimensions={0}, use_global_device_ids=true | all-gather | bytes 100 | tf_op jit(solution)/shard_map/all_gather | solution.py:51
  38.4 0.8 copy.71
  39.2 1.1 slice_reduce_fusion.2
  42.1 1.8 fusion.14
  44.0 1.1 fusion.39
  45.1 11.1 %all_gather.38 = bf16[4,10,64,128]{3,2,1,0:T(8,128)(2,1)S(1)} all-gather(bf16[1,10,64,128]{3,2,1,0:T(8,128)(2,1)S(1)} %get-tuple-element.22), channel_id=1, replica_groups=mesh['seq_0'=8,'seq_1'=4,'head_0'=4,'head_1'=2] {'seq_1'}, dimensions={0}, use_global_device_ids=true | all-gather | bytes 819200 | tf_op jit(solution)/shard_map/all_gather | solution.py:51
  56.3 0.8 copy-done.2
  57.1 0.9 fusion.41
  58.9 1.4 copy.64
  61.0 2.2 fusion.78
  63.2 1.4 copy.73
  65.1 15.0 %all-gather.2 = bf16[8,1,10]{2,1,0:T(2,128)(2,1)S(1)} all-gather(bf16[1,1,10]{2,1,0:T(2,128)(2,1)S(1)} %get-tuple-element.53), channel_id=1, replica_groups=mesh['seq_0'=8,'seq_1'=4,'head_0'=4,'head_1'=2] {'seq_0'}, dimensions={0}, use_global_device_ids=true | all-gather | bytes 180 | tf_op jit(solution)/shard_map/all_gather | solution.py:51
  81.3 16.2 %all-gather.9.cloned.1.call-done = bf16[8,10,64,128]{3,2,1,0:T(8,128)(2,1)} async-done(((bf16[1,10,64,128]{3,2,1,0:T(8,128)(2,1)}), bf16[8,10,64,128]{3,2,1,0:T(8,128)(2,1)}) %all-gather.9.cloned.1.call-update) | async-done | bytes 1310736 | tf_op jit(solution)/shard_map/all_gather | solution.py:51
  97.5 3.4 %fusion.76 = (bf16[1,10,64,128]{3,2,1,0:T(8,128)(2,1)}, f32[1,10,64,128]{3,2,1,0:T(8,128)}) fusion(pred[]{:T(512)S(6)} %gt.39, pred[]{:T(512)S(6)} %gt.38, pred[]{:T(512)S(6)} %gt.37, bf16[4,10,64,128]{3,2,1,0:T(8,128)(2,1)} %copy-done.2, f32[10]{0:T(128)} %copy-done.38, f32[10]{0:T(128)} %copy-done.25, f32[10]{0:T(128)S(1)} %get-tuple-element.55, ...), kind=kLoop, calls=%fused_computation.162 | loop fusion | flops 4014080 | bytes 2458132 | tf_op jit(solution)/shard_map/convert.22
  101.0 22.5 %all-gather.11.cloned.1.call-done = bf16[8,128,2560]{2,1,0:T(8,128)(2,1)} async-done(((bf16[4,128,2560]{2,1,0:T(8,128)(2,1)}), bf16[8,128,2560]{2,1,0:T(8,128)(2,1)}) %all-gather.11.cloned.1.call-update) | async-done | bytes 5242896 | tf_op jit(solution)/shard_map/all_gather | solution.py:28
  123.4 3.1 %copy.76 = bf16[4,2,128,2560]{3,2,1,0:T(8,128)(2,1)S(1)} copy(bf16[4,2,128,2560]{3,2,0,1:T(8,128)(2,1)} %bitcast.206) | data formatting | bytes 10485760 | tf_op jit(solution)/shard_map/transpose | solution.py:32
  126.6 5.4 %multiply_convert_fusion.3 = bf16[1024,640]{1,0:T(8,128)(2,1)} fusion(bf16[1024,2560]{1,0:T(8,128)(2,1)S(1)} %bitcast.207, bf16[640,2560]{1,0:T(8,128)(2,1)S(1)} %copy-done, bf16[1024,640]{1,0:T(8,128)(2,1)S(1)} %copy-done.42), kind=kOutput, calls=%fused_computation.22 | convolution fusion | flops 3360030720 | bytes 11141120 | tf_op jit(solution)/shard_map/dot_general | solution.py:128
  132.0 2.5 %copy.77 = bf16[1024,640]{0,1:T(8,128)(2,1)} copy(bf16[1024,640]{1,0:T(8,128)(2,1)} %multiply_convert_fusion.3) | data formatting | bytes 2621440 | tf_op jit(solution)/shard_map/convert_element_type | solution.py:134
  134.5 3.8 %reshape.404 = bf16[4,256,10,64]{1,0,3,2:T(4,128)(2,1)} reshape(bf16[1024,640]{0,1:T(8,128)(2,1)} %copy.77) | data formatting | bytes 2621440 | tf_op jit(solution)/shard_map/reshape | solution.py:135
  138.4 2.0 fusion.12
  140.5 1.2 add_convert_fusion.5
  141.7 11.3 %all_gather.43 = bf16[4,10,64,128]{3,2,1,0:T(8,128)(2,1)S(1)} all-gather(bf16[1,10,64,128]{3,2,1,0:T(8,128)(2,1)S(1)} %get-tuple-element.58), channel_id=1, replica_groups=mesh['seq_0'=8,'seq_1'=4,'head_0'=4,'head_1'=2] {'seq_1'}, dimensions={0}, use_global_device_ids=true | all-gather | bytes 819200 | tf_op jit(solution)/shard_map/all_gather | solution.py:51
  153.0 0.8 copy-done.1
  153.9 0.9 fusion.40
  155.1 1.2 compare_and_fusion
  156.4 1.8 fusion.22
  158.2 4.1 %fusion.3 = f32[4,256,10,64]{1,3,2,0:T(8,128)S(1)} fusion(f32[4,10,64,256]{3,2,1,0:T(8,128)S(1)} %fusion.22, f32[4,256,256]{2,1,0:T(8,128)S(1)} %copy-done.11, f32[4,10,256]{2,1,0:T(8,128)S(1)} %copy-done.22, pred[4,256,256]{2,1,0:T(8,128)(4,1)S(1)} %compare_and_fusion, f32[10]{0:T(128)} %param.14, f32[4,256,10]{1,2,0:T(8,128)S(1)} %copy-done.24, ...), kind=kOutput, calls=%fused_computation.11 | convolution fusion | flops 351928320 | bytes 7946280 | tf_op jit(solution)/shard_map/khts,kshp->kthp/dot_general | solution.py:109
  162.3 1.7 copy.74
  164.0 2.1 copy.84
  166.1 3.2 %copy.75 = f32[1024,640]{1,0:T(8,128)} copy(f32[1024,640]{0,1:T(8,128)} %bitcast.205) | data formatting | bytes 5242880 | tf_op jit(solution)/shard_map/reshape | solution.py:167
  169.3 8.8 %convolution_convert_fusion = bf16[1024,2560]{1,0:T(8,128)(2,1)} fusion(bf16[640,2560]{1,0:T(8,128)(2,1)S(1)} %copy-done, f32[1024,640]{1,0:T(8,128)} %copy.75, bf16[1024,640]{1,0:T(8,128)(2,1)} %param.10), kind=kOutput, calls=%fused_computation.1 | convolution fusion | flops 3362652160 | bytes 12451840 | tf_op jit(solution)/shard_map/dot_general | solution.py:169
  178.2 14.3 %all-gather.3 = bf16[8,1,10]{2,1,0:T(2,128)(2,1)S(1)} all-gather(bf16[1,1,10]{2,1,0:T(2,128)(2,1)} %get-tuple-element.52), channel_id=1, replica_groups=mesh['seq_0'=8,'seq_1'=4,'head_0'=4,'head_1'=2] {'seq_0'}, dimensions={0}, use_global_device_ids=true | all-gather | bytes 180 | tf_op jit(solution)/shard_map/all_gather | solution.py:51
  193.6 2.8 %add_convert_fusion.2 = (bf16[1,10,64,128]{3,2,1,0:T(8,128)(2,1)S(1)}, f32[1,10,64,128]{3,2,1,0:T(8,128)S(1)}) fusion(f32[10]{0:T(128)} %get-tuple-element.14, f32[1,10,64,128]{3,2,1,0:T(8,128)} %get-tuple-element.59, f32[10]{0:T(128)S(1)} %get-tuple-element.10, f32[4,10,64,128]{3,2,1,0:T(8,128)} %copy-done.3, pred[]{:T(512)S(6)} %lt.39, pred[]{:T(512)S(6)} %lt.38, ...), kind=kLoop, calls=%fused_computation.61 | loop fusion | flops 4341760 | bytes 3113572 | tf_op jit(solution)/shard_map/convert.18
  196.5 1.3 add_convert_fusion.1
  198.4 3.6 %fusion.9 = bf16[4,256,10,64]{1,3,2,0:T(8,128)(2,1)S(1)} fusion(f32[4,10,64,256]{3,2,1,0:T(8,128)S(1)} %fusion.30, f32[4,256,256]{2,1,0:T(8,128)S(1)} %copy-done.12, f32[4,10,256]{2,1,0:T(8,128)S(1)} %copy-done.23, pred[4,256,256]{2,1,0:T(8,128)(4,1)S(1)} %copy-done.19, f32[10]{0:T(128)S(1)} %copy-done.43, f32[4,256,10]{1,2,0:T(8,128)S(1)} %copy-done.21, ...), kind=kOutput, calls=%fused_computation.17 | convolution fusion | flops 352583680 | bytes 6635560 | tf_op jit(solution)/shard_map/khts,kthp->kshp/dot_general | solution.py:136
  202.0 1.0 copy.80
  203.0 1.4 copy.85
  204.4 2.4 copy.81
  206.8 31.8 %reduce-scatter.2.cloned.1.call-done = bf16[128,2560]{1,0:T(8,128)(2,1)} async-done(((bf16[1024,2560]{1,0:T(8,128)(2,1)}), bf16[128,2560]{1,0:T(8,128)(2,1)}) %reduce-scatter.2.cloned.1.call-update) | async-done | bytes 655376 | tf_op jit(solution)/shard_map/reduce_scatter | solution.py:168
  (127 shorter events, 9.6 us)
Async XLA Ops:
  7.2 119.4 %copy-start = (bf16[640,2560]{1,0:T(8,128)(2,1)S(1)}, bf16[640,2560]{1,0:T(8,128)(2,1)}, u32[]{:S(2)}) copy-start(bf16[640,2560]{1,0:T(8,128)(2,1)} %param.16) | copy-start | bytes 9830404
  7.2 51.0 %all-gather.15.cloned.1.call-start = ((), (), s32[]{:S(2)}) async-start(), calls=%async_computation.5 | async-start | bytes 3276800 | tf_op jit(solution)/shard_map/all_gather | solution.py:28
  7.9 89.6 %all-gather.9.cloned.1.call-start = ((), (), s32[]{:S(2)}) async-start(), calls=%async_computation.1 | async-start | bytes 1474560 | tf_op jit(solution)/shard_map/all_gather | solution.py:51
  10.1 12.6 %collective-permute-start = (s32[1]{0:T(128)}, s32[1]{0:T(128)}, u32[]{:S(2)}, u32[]{:S(2)}) collective-permute-start(s32[1]{0:T(128)} %add.280), channel_id=1, source_target_pairs={{0,8},{8,16},{16,24},{24,32},{32,40},{40,48},{48,56},{56,64},{64,7... | collective-permute-start | bytes 20 | tf_op jit(solution)/shard_map/ppermute | solution.py:16
  19.8 22.3 %copy-start.14 = (bf16[1024,128]{1,0:T(8,128)(2,1)S(1)}, bf16[1024,128]{1,0:T(8,128)(2,1)}, u32[]{:S(2)}) copy-start(bf16[1024,128]{1,0:T(8,128)(2,1)} %param.11) | copy-start | bytes 786436
  39.2 17.1 %copy-start.20 = (f32[4,256,10]{1,2,0:T(8,128)}, f32[4,256,10]{1,2,0:T(8,128)S(1)}, u32[]{:S(2)}) copy-start(f32[4,256,10]{1,2,0:T(8,128)S(1)} %copy.71) | copy-start | bytes 122884
  40.3 1.8 copy-start.36
  40.3 16.0 %copy-start.27 = (f32[10]{0:T(128)}, f32[10]{0:T(128)S(1)}, u32[]{:S(2)}) copy-start(f32[10]{0:T(128)S(1)} %get-tuple-element.11) | copy-start | bytes 124
  40.3 15.9 %copy-start.29 = (f32[10]{0:T(128)}, f32[10]{0:T(128)S(1)}, u32[]{:S(2)}) copy-start(f32[10]{0:T(128)S(1)} %get-tuple-element.8) | copy-start | bytes 124
  40.9 15.4 %copy-start.25 = (f32[10]{0:T(128)}, f32[10]{0:T(128)S(1)}, u32[]{:S(2)}) copy-start(f32[10]{0:T(128)S(1)} %get-tuple-element.56) | copy-start | bytes 124
  40.9 15.4 %copy-start.39 = (f32[10]{0:T(128)}, f32[10]{0:T(128)S(1)}, u32[]{:S(2)}) copy-start(f32[10]{0:T(128)S(1)} %get-tuple-element.57) | copy-start | bytes 124
  41.5 14.8 %copy-start.38 = (f32[10]{0:T(128)}, f32[10]{0:T(128)S(1)}, u32[]{:S(2)}) copy-start(f32[10]{0:T(128)S(1)} %get-tuple-element.49) | copy-start | bytes 124
  42.1 14.1 %copy-start.33 = (f32[10]{0:T(128)}, f32[10]{0:T(128)S(1)}, u32[]{:S(2)}) copy-start(f32[10]{0:T(128)S(1)} %get-tuple-element.62) | copy-start | bytes 124
  44.0 1.2 copy-start.4
  45.1 15.8 %copy-start.13 = (bf16[1024,128]{1,0:T(8,128)(2,1)S(1)}, bf16[1024,128]{1,0:T(8,128)(2,1)}, u32[]{:S(2)}) copy-start(bf16[1024,128]{1,0:T(8,128)(2,1)} %param.12) | copy-start | bytes 786436
  56.3 0.8 copy-start.2
  58.1 65.3 %all-gather.11.cloned.1.call-start = ((), (), s32[]{:S(2)}) async-start(), calls=%async_computation.3 | async-start | bytes 7864320 | tf_op jit(solution)/shard_map/all_gather | solution.py:28
  58.8 134.8 %all-gather.13.cloned.1.call-start = ((), (), s32[]{:S(2)}) async-start(), calls=%async_computation.4 | async-start | bytes 1474560 | tf_op jit(solution)/shard_map/all_gather | solution.py:51
  123.4 3.2 %copy-start.42 = (bf16[1024,640]{1,0:T(8,128)(2,1)S(1)}, bf16[1024,640]{1,0:T(8,128)(2,1)}, u32[]{:S(2)}) copy-start(bf16[1024,640]{1,0:T(8,128)(2,1)} %param.10) | copy-start | bytes 3932164
  138.3 2.1 copy-start.5
  138.3 2.1 copy-start.9
  138.3 2.1 copy-start.10
  138.3 2.1 copy-start.30
  138.3 2.1 copy-start.31
  138.3 2.1 copy-start.34
  138.4 2.1 copy-start.37
  138.4 2.1 copy-start.40
  138.4 2.1 copy-start.41
  140.4 1.3 copy-start.3
  140.4 13.5 %copy-start.26 = (f32[10]{0:T(128)S(1)}, f32[10]{0:T(128)}, u32[]{:S(2)}) copy-start(f32[10]{0:T(128)} %copy-done.25) | copy-start | bytes 124
  140.4 13.5 %copy-start.32 = (f32[10]{0:T(128)S(1)}, f32[10]{0:T(128)}, u32[]{:S(2)}) copy-start(f32[10]{0:T(128)} %get-tuple-element.50) | copy-start | bytes 124
  140.4 13.5 %copy-start.35 = (f32[10]{0:T(128)S(1)}, f32[10]{0:T(128)}, u32[]{:S(2)}) copy-start(f32[10]{0:T(128)} %get-tuple-element.54) | copy-start | bytes 124
  153.0 0.8 copy-start.1
  154.8 83.8 %reduce-scatter.2.cloned.1.call-start = ((), (), s32[]{:S(2)}) async-start(), calls=%async_computation.2 | async-start | bytes 5898240 | tf_op jit(solution)/shard_map/reduce_scatter | solution.py:168
  155.1 3.1 %copy-start.7 = (bf16[4,256,10,64]{1,0,3,2:T(4,128)(2,1)S(1)}, bf16[4,256,10,64]{1,0,3,2:T(4,128)(2,1)}, u32[]{:S(2)}) copy-start(bf16[4,256,10,64]{1,0,3,2:T(4,128)(2,1)} %reshape.401) | copy-start | bytes 3932164
  155.1 3.1 %copy-start.11 = (f32[4,256,256]{2,1,0:T(8,128)S(1)}, f32[4,256,256]{2,1,0:T(8,128)}, u32[]{:S(2)}) copy-start(f32[4,256,256]{2,1,0:T(8,128)} %fusion.78) | copy-start | bytes 3145732
  155.1 3.1 %copy-start.22 = (f32[4,10,256]{2,1,0:T(8,128)S(1)}, f32[4,10,256]{2,1,0:T(8,128)}, u32[]{:S(2)}) copy-start(f32[4,10,256]{2,1,0:T(8,128)} %copy.64) | copy-start | bytes 122884
  155.1 3.1 %copy-start.24 = (f32[4,256,10]{1,2,0:T(8,128)S(1)}, f32[4,256,10]{1,2,0:T(8,128)}, u32[]{:S(2)}) copy-start(f32[4,256,10]{1,2,0:T(8,128)} %copy.73) | copy-start | bytes 122884
  156.4 5.9 %copy-start.18 = (pred[4,256,256]{2,1,0:T(8,128)(4,1)}, pred[4,256,256]{2,1,0:T(8,128)(4,1)S(1)}, u32[]{:S(2)}) copy-start(pred[4,256,256]{2,1,0:T(8,128)(4,1)S(1)} %compare_and_fusion) | copy-start | bytes 786436
  178.1 18.3 %copy-start.28 = (f32[10]{0:T(128)S(1)}, f32[10]{0:T(128)}, u32[]{:S(2)}) copy-start(f32[10]{0:T(128)} %copy-done.27) | copy-start | bytes 124
  178.1 19.6 %copy-start.15 = (bf16[1024,128]{1,0:T(8,128)(2,1)S(1)}, bf16[1024,128]{1,0:T(8,128)(2,1)}, u32[]{:S(2)}) copy-start(bf16[1024,128]{1,0:T(8,128)(2,1)} %param.11) | copy-start | bytes 786436
  193.6 2.8 %copy-start.6 = (f32[1,10,64,128]{3,2,1,0:T(8,128)S(1)}, f32[1,10,64,128]{3,2,1,0:T(8,128)}, u32[]{:S(2)}) copy-start(f32[1,10,64,128]{3,2,1,0:T(8,128)} %get-tuple-element.59) | copy-start | bytes 983044
  196.4 1.9 copy-start.8
  196.4 1.9 copy-start.12
  196.4 1.9 copy-start.19
  196.4 1.9 copy-start.21
  196.4 1.9 copy-start.23
  196.4 1.9 copy-start.43
  (2 other events, 1.2 us)
Sparse Core Ops, SparseCore 0:
  9.8 41.4 all-gather.14
  58.2 39.2 all-gather.8
  99.3 24.0 all-gather.10
  155.0 36.9 all-gather.12
  194.9 43.6 reduce-scatter.1
where the time goes:
time: 248 us; the launch traced here: 245 us
  waiting for transfers between devices  72 us (29%)
  blocking collectives  60.5 us (24%)
  local copies, waits for them, and re-layouts  39.4 us (16%)
  matrix products  30.2 us (12%)
  other arithmetic  22.3 us (9%)
  between operations  15.8 us (6%)
  starting transfers between devices  5.11 us (2%)
    all_gather x5, blocking collectives, entering_2(): lax.all_gather(part.astype(kind), axis)  60.5 us
    reduce_scatter x1, waiting for transfers between devices, shards(): lax.psum_scatter(jnp.dot(gated, out_weight, preferred_element_type=jnp.fl...  31.8 us
    all_gather x2, waiting for transfers between devices, gather_in_order(): pieces = lax.all_gather(pieces, axes[k], axis=0, tiled=True)  22.5 us
    all_gather x2, waiting for transfers between devices, entering_2(): lax.all_gather(part.astype(kind), axis)  16.2 us
    unnamed x92, local copies, waits for them, and re-layouts  11.3 us
    another operation x7, other arithmetic  11.1 us
    dot_general x1, matrix products, shards(): jnp.dot(gated, out_weight, preferred_element_type=jnp.float32)  8.79 us
    dot_general x1, matrix products, shards(): lax.dot_general(whole_of(grad_out, HEAD, (0, 1), 0), out_weight, (((1,),...  5.44 us
  transfers between devices with their start and end apart: 6, of which 3 were waited for; matrix products, arithmetic and copies ran while one was open for 29% of the time, Pallas kernels for 0%

commit v1 on v0

v1 whole, which is shorter than its diff:
```python
import math

import jax
import jax.numpy as jnp
from jax import lax
from jax.experimental import pallas as pl
from jax.experimental.pallas import tpu as pltpu
from jax.sharding import PartitionSpec as P

NX, NY, NZ = 4, 4, 8
Q = 128
CHUNKS = 8
TOK = Q * CHUNKS
HEADS = 10
PAIRS = 5
HP = 64
WIDTH = HEADS * HP
N = 128
D = 2560
QR = N // NY
HALF = 64
LOG2E = 1.0 / math.log(2.0)
MESH = pl.DeviceIdType.MESH
BF = jnp.bfloat16
F32 = jnp.float32


def dot(a, b):
    return jnp.dot(a, b, preferred_element_type=F32)


def dot_nt(a, b):
    return lax.dot_general(a, b, (((1,), (1,)), ((), ())), preferred_element_type=F32)


def dot_tn(a, b):
    return lax.dot_general(a, b, (((0,), (0,)), ((), ())), preferred_element_type=F32)


def split3(v):
    a = v.astype(BF)
    rest = v - a.astype(F32)
    b = rest.astype(BF)
    return a, b, (rest - b.astype(F32)).astype(BF)


def stacked(rows, count):
    place = lax.broadcasted_iota(jnp.int32, (count, 128), 0)
    out = jnp.zeros((count, 128), F32)
    for k, row in enumerate(rows):
        out = jnp.where(place == k, row, out)
    return out


def kernel(
    x_hbm, g_hbm, wk, rk, ld, skip, docs, wo_hbm, go_hbm,
    mo, gi,
    x_v, g_v, wo_v, go_v, silu_v, mix_v, gl_v, exc_v, enc_v, exs_v, ens_v, wt_v, dy_v,
    enter_v, arr_v, own_v, run_v, ldp_v, ccol_v, crow_v, dt_v, bd_v, off_v, prev_v, spread_v,
    y1s, y1r, m1s, m1r, zs, zr, mzs, mzr, y2s, y2r, wrow_v, brow_v, zrow_v,
    b1s, b1r, bzs, bzr, b2s, b2r,
    pall, pr, qs, rla, rlb, fl, fr,
    lsem, agx_s, agx_r, agd_s, agd_r,
    y1_ss, y1_rs, m1_ss, m1_rs, z_ss, z_rs, mz_ss, mz_rs, y2_ss, y2_rs,
    b1_ss, b1_rs, bz_ss, bz_rs, b2_ss, b2_rs,
    d_ss, d_rs, rx_ss, rx_rs,
):
    seq = lax.axis_index("seq")
    head = lax.axis_index("head")
    z, y = seq // NY, seq % NY
    xx, core = head // 2, head % 2
    x_at = lambda k: (xx + k) % NX

    def dev(seq_id, head_id):
        return {"seq": seq_id, "head": head_id}

    right = dev(seq, x_at(1) * 2 + core)
    left = dev(seq, x_at(3) * 2 + core)
    partner = dev(seq, xx * 2 + 1 - core)
    y_peer = lambda r: dev(z * NY + (y + r) % NY, head)
    z_peer = lambda r: dev(((z + r) % NZ) * NY + y, head)

    def remote(src, dst, ss, rs, to):
        return pltpu.make_async_remote_copy(
            src_ref=src, dst_ref=dst, send_sem=ss, recv_sem=rs, device_id=to, device_id_type=MESH
        )

    started = []

    def send(*args):
        copy = remote(*args)
        copy.start()
        started.append(copy)

    own_rows = pl.ds(pl.multiple_of(head * Q, Q), Q)
    loads = [
        pltpu.make_async_copy(go_hbm, go_v.at[own_rows, :], lsem.at[0]),
        pltpu.make_async_copy(x_hbm, x_v, lsem.at[1]),
        pltpu.make_async_copy(g_hbm, g_v, lsem.at[2]),
        pltpu.make_async_copy(wo_hbm, wo_v, lsem.at[3]),
    ]
    for copy in loads:
        copy.start()

    barrier = pltpu.get_barrier_semaphore()
    peers = [right, left, partner]
    peers += [y_peer(r) for r in range(1, NY)] + [z_peer(r) for r in range(1, NZ)]
    for peer in peers:
        pl.semaphore_signal(barrier, inc=1, device_id=peer, device_id_type=MESH)
    pl.semaphore_wait(barrier, len(peers))

    def go_rows(place, of_core, half):
        start = pl.multiple_of((place * 2 + of_core) * Q + half * HALF, HALF)
        return go_v.at[pl.ds(start, HALF), :]

    loads[0].wait()
    for half in (0, 1):
        ref = go_rows(xx, core, half)
        send(ref, ref, agx_s.at[half], agx_r.at[half], right)
    for half in (1, 0):
        ref = go_rows(xx, core, half)
        send(ref, ref, agx_s.at[2 + half], agx_r.at[2 + half], left)
    own_ref = go_v.at[own_rows, :]
    send(own_ref, own_ref, agd_s.at[6], agd_r.at[6], partner)

    def ag_got(unit):
        place = x_at((3, 3, 1, 1, 2, 2)[unit])
        ref = go_rows(place, core, unit % 2)
        remote(ref, ref, agx_s.at[unit], agx_r.at[unit], left).wait_recv()
        if unit == 0:
            send(ref, ref, agx_s.at[4], agx_r.at[4], right)
        if unit == 3:
            send(ref, ref, agx_s.at[5], agx_r.at[5], left)
        send(ref, ref, agd_s.at[unit], agd_r.at[unit], partner)

    def ag_pair_got(unit):
        place = x_at((3, 3, 1, 1, 2, 2)[unit])
        ref = go_rows(place, 1 - core, unit % 2)
        remote(ref, ref, agd_s.at[unit], agd_r.at[unit], partner).wait_recv()

    sub = lax.broadcasted_iota(jnp.int32, (Q, Q), 0)
    lane = lax.broadcasted_iota(jnp.int32, (Q, Q), 1)
    tri = (lane <= sub).astype(F32).astype(BF)
    eye = (lane == sub).astype(F32).astype(BF)
    head_lane = lax.broadcasted_iota(jnp.int32, (1, 128), 1)
    lane_row = (lax.broadcasted_iota(jnp.int32, (128, WIDTH), 1) // HP)
    head_row = lax.broadcasted_iota(jnp.int32, (128, WIDTH), 0)
    spread_v[...] = (lane_row == head_row).astype(F32).astype(BF)
    m_lo = (head_lane < HP).astype(F32).astype(BF)
    m_hi = (head_lane >= HP).astype(F32).astype(BF)

    def expand(w):
        return dot(w.astype(BF), spread_v[...])

    def expand_fine(w):
        a = w.astype(BF)
        return dot(a, spread_v[...]) + dot((w - a.astype(F32)).astype(BF), spread_v[...])

    def rows_of(c):
        return pl.ds(pl.multiple_of(c * Q, Q), Q)

    ldp_v[...] = jnp.zeros_like(ldp_v)
    ldp_v[0:HEADS, :] = ld[...] * LOG2E
    doc_f = docs[...].astype(F32)
    df = jnp.broadcast_to(doc_f[0:1, 0:1], (1, 128))
    off_v[...] = jnp.zeros_like(off_v)
    prev_v[...] = jnp.broadcast_to(df, prev_v.shape)
    run_v[...] = jnp.zeros_like(run_v)
    loads[1].wait()

    @pl.loop(0, CHUNKS)
    def _(c):
        rows = rows_of(c)
        cols = rows_of(c)
        parts = split3(ldp_v[:, cols])
        ccol = sum(dot_nt(tri, part) for part in parts)
        ccol_v[rows, :] = ccol
        crow_v[c] = sum(dot_nt(part[0:16], tri) for part in parts)
        doc_row = docs[pl.ds(c, 1), :].astype(F32)
        dt = dot_nt(eye, jnp.broadcast_to(doc_row, (Q, Q)).astype(BF))
        dt_v[rows, :] = dt
        c_end, d_end = ccol[Q - 1 : Q, :], dt[Q - 1 : Q, :]
        exc = expand(jnp.where(dt == d_end, jnp.exp2(c_end - ccol), 0.0)).astype(BF)
        exc_v[rows, :] = exc
        prev = prev_v[0:1, :]
        bd = jnp.where(d_end == prev, jnp.exp2(c_end), 0.0)
        bdx = expand_fine(jnp.broadcast_to(bd, (8, 128)))
        bd_v[c] = bdx
        own = dot_tn(wk[rows, :], x_v[rows, :] * exc)
        run = run_v[...]
        enter_v[c] = run.astype(BF)
        run_v[...] = run * bdx[0:1, :] + own
        entw = jnp.where(dt == prev, jnp.exp2(ccol), 0.0)
        enc_v[rows, :] = expand(entw).astype(BF)
        off = off_v[0:1, :]
        ens_v[rows, :] = expand(jnp.where(dt == df, jnp.exp2(ccol + off), 0.0)).astype(BF)
        prev_v[...] = jnp.broadcast_to(d_end, prev_v.shape)
        off_v[...] = jnp.broadcast_to(off + c_end, off_v.shape)

    total = off_v[0:1, :]
    dl = prev_v[0:1, :]
    y1s[...] = run_v[...].astype(BF)
    m1s[...] = stacked([total, df, dl], 8)
    own_q = pl.ds(pl.multiple_of(y * QR, QR), QR)
    m1r[y] = m1s[...]
    y1r[y] = y1s[own_q, :]
    for r in range(1, NY):
        q_rows = pl.ds(pl.multiple_of(((y + r) % NY) * QR, QR), QR)
        send(m1s, m1r.at[y], m1_ss.at[r], m1_rs.at[r], y_peer(r))
        send(y1s.at[q_rows, :], y1r.at[y], y1_ss.at[r], y1_rs.at[r], y_peer(r))

    skip_rows = [
        jnp.where(head_lane < HP, skip[2 * p], skip[2 * p + 1]) for p in range(PAIRS)
    ]

    def pair(p):
        return slice(p * 128, (p + 1) * 128)

    def doubled(v):
        return jnp.concatenate([v * m_lo, v * m_hi], axis=0)

    def inner_chunk(c):
        rows = rows_of(c)
        ccol, dt = ccol_v[rows, :], dt_v[rows, :]
        crow = crow_v[c]
        same = dt == docs[pl.ds(c, 1), :].astype(F32)
        b, k = wk[rows, :], rk[rows, :]
        sm = jnp.where(same & (sub >= lane), dot_nt(k, b), 0.0)
        stm = jnp.where(same & (lane >= sub), dot_nt(b, k), 0.0)
        off_c = off_v[0:1, :]
        shard_c = ccol + off_c
        exs = jnp.where(dt == dl, jnp.exp2(total - shard_c), 0.0)
        exs_v[rows, :] = expand(exs).astype(BF)
        for p in range(PAIRS):
            ws, wts = [], []
            for h in (2 * p, 2 * p + 1):
                gap = ccol[:, h : h + 1] - crow[h : h + 1, :]
                ws.append((jnp.exp2(jnp.minimum(gap, 0.0)) * sm).astype(BF))
                wts.append((jnp.exp2(jnp.minimum(-gap, 0.0)) * stm).astype(BF))
            wt_v[c, p] = jnp.concatenate(wts, axis=1)
            xp = x_v[rows, pair(p)]
            mixed = dot(jnp.concatenate(ws, axis=1), doubled(xp))
            mixed += enc_v[rows, pair(p)].astype(F32) * dot(k, enter_v[c, :, pair(p)])
            mix_v[rows, pair(p)] = mixed + skip_rows[p] * xp.astype(F32)
            gate = g_v[rows, pair(p)].astype(F32)
            silu_v[rows, pair(p)] = gate / (1.0 + jnp.exp(-gate))
        off_v[...] = jnp.broadcast_to(off_c + ccol[Q - 1 : Q, :], off_v.shape)

    off_v[...] = jnp.zeros_like(off_v)
    loads[2].wait()
    pl.loop(0, 4)(inner_chunk)

    for r in range(1, NY):
        source = (y + NY - r) % NY
        remote(m1s, m1r.at[source], m1_ss.at[r], m1_rs.at[r], y_peer(r)).wait_recv()
        remote(y1s.at[own_q, :], y1r.at[source], y1_ss.at[r], y1_rs.at[r], y_peer(r)).wait_recv()
    meta = [m1r[j] for j in range(NY)]
    ls = [m[0:1, :] for m in meta]
    dfs = [m[1:2, :] for m in meta]
    dls = [m[2:3, :] for m in meta]

    def span(values):
        out = jnp.zeros((1, 128), F32)
        for v in values:
            out = out + v
        return out

    def gated_decay(a, b, values):
        return jnp.where(a == b, jnp.exp2(span(values)), 0.0)

    t_rows = [gated_decay(dls[j], dls[NY - 1], ls[j + 1 :]) for j in range(NY)]
    t_rows += [gated_decay(dfs[j], dfs[0], ls[:j]) for j in range(NY)]
    zrow_v[...] = expand_fine(stacked(t_rows, 8))
    zs[...] = sum(zrow_v[j : j + 1, :] * y1r[j].astype(F32) for j in range(NY)).astype(BF)
    mzs[...] = stacked([span(ls), dfs[0], dls[NY - 1]], 8)
    zr[z] = zs[...]
    mzr[z] = mzs[...]
    for r in range(1, NZ):
        send(mzs, mzr.at[z], mz_ss.at[r], mz_rs.at[r], z_peer(r))
        send(zs, zr.at[z], z_ss.at[r], z_rs.at[r], z_peer(r))

    in_row = [(j, k) for k in range(NY) for j in range(k)]
    f_rows = [gated_decay(dls[j], dfs[k], ls[j + 1 : k]) for j, k in in_row]
    f_rows += [gated_decay(dfs[0], dfs[k], ls[:k]) for k in range(NY)]
    wrow_v[...] = expand_fine(stacked(f_rows, 16))
    b_rows = [gated_decay(dfs[k], dls[j], ls[j + 1 : k]) for j, k in in_row]
    b_rows += [gated_decay(dls[NY - 1], dls[k], ls[k + 1 :]) for k in range(NY)]
    brow_v[...] = expand_fine(stacked(b_rows, 16))

    ag_got(0)
    ag_got(3)

    pl.loop(4, CHUNKS)(inner_chunk)

    loads[3].wait()

    def grad_mix_of(place):
        rows = pl.ds(pl.multiple_of(place * 2 * Q, 2 * Q), 2 * Q)
        grad = dot_nt(go_v[rows, :], wo_v[...])
        dy_v[rows, :] = (grad * silu_v[rows, :]).astype(BF)
        for k in (0, 1):
            c = place * 2 + k
            one = rows_of(c)
            own_v[c] = dot_tn(rk[one, :], dy_v[one, :] * enc_v[one, :])

    pair_own = go_v.at[pl.ds(pl.multiple_of((xx * 2 + 1 - core) * Q, Q), Q), :]
    remote(pair_own, pair_own, agd_s.at[6], agd_r.at[6], partner).wait_recv()
    grad_mix_of(xx)

    ag_got(1)
    ag_got(2)

    for r in range(1, NZ):
        source = (z + NZ - r) % NZ
        remote(mzs, mzr.at[source], mz_ss.at[r], mz_rs.at[r], z_peer(r)).wait_recv()
        remote(zs, zr.at[source], z_ss.at[r], z_rs.at[r], z_peer(r)).wait_recv()
    zmeta = [mzr[i] for i in range(NZ)]
    rls = [m[0:1, :] for m in zmeta]
    rdfs = [m[1:2, :] for m in zmeta]
    rdls = [m[2:3, :] for m in zmeta]

    def flag(condition):
        return jnp.where(condition, 1.0, 0.0).astype(F32)

    zf_rows, zb_rows = [], []
    for i in range(NZ):
        gap = span([rls[m] * flag(m < z) for m in range(i + 1, NZ)])
        zf_rows.append(flag(i < z) * jnp.where(rdls[i] == dfs[0], jnp.exp2(gap), 0.0))
        gap = span([rls[m] * flag(m > z) for m in range(i)])
        zb_rows.append(flag(i > z) * jnp.where(rdfs[i] == dls[NY - 1], jnp.exp2(gap), 0.0))
    zf = expand_fine(stacked(zf_rows, 8))
    row_state = sum(zf[i : i + 1, :] * zr[i].astype(F32) for i in range(NZ))
    for k in range(NY):
        out = wrow_v[6 + k : 7 + k, :] * row_state
        for place, (j, kk) in enumerate(in_row):
            if kk == k:
                out += wrow_v[place : place + 1, :] * y1r[j].astype(F32)
        y2s[k * QR : (k + 1) * QR, :] = out.astype(BF)
    y2r[own_q, :] = y2s[own_q, :]
    for r in range(1, NY):
        q_rows = pl.ds(pl.multiple_of(((y + r) % NY) * QR, QR), QR)
        send(y2s.at[q_rows, :], y2r.at[own_q, :], y2_ss.at[r], y2_rs.at[r], y_peer(r))
    zrow_b = expand_fine(stacked(zb_rows, 8))

    ag_pair_got(0)
    ag_pair_got(1)
    grad_mix_of(x_at(3))
    ag_pair_got(2)
    ag_pair_got(3)
    grad_mix_of(x_at(1))

    for r in range(1, NY):
        source = pl.ds(pl.multiple_of(((y + NY - r) % NY) * QR, QR), QR)
        remote(y2s.at[own_q, :], y2r.at[source, :], y2_ss.at[r], y2_rs.at[r], y_peer(r)).wait_recv()

    order = [x_at(2), x_at(1), x_at(3), xx]
    mine = pl.ds(pl.multiple_of(core * Q, Q), Q)
    theirs = pl.ds(pl.multiple_of((1 - core) * Q, Q), Q)

    def project(k):
        rows = pl.ds(pl.multiple_of(order[k] * 2 * Q, 2 * Q), 2 * Q)
        carried = ens_v[rows, :].astype(F32) * dot(rk[rows, :], y2r[...])
        gated = ((mix_v[rows, :] + carried) * silu_v[rows, :]).astype(BF)
        for n in range(5):
            cols = slice(n * 512, (n + 1) * 512)
            pall[k, :, cols] = dot(gated, wo_v[:, cols]).astype(BF)
        send(pall.at[k, theirs, :], pr.at[k], d_ss.at[k], d_rs.at[k], partner)

    def pair_sum(k, start, count):
        rows = pl.ds(pl.multiple_of(core * Q + start, HALF), count)
        return pall[k, rows, :].astype(F32) + pr[k, start : start + count, :].astype(F32)

    def pair_got(k):
        remote(pall.at[k, mine, :], pr.at[k], d_ss.at[k], d_rs.at[k], partner).wait_recv()

    def half(ref, which):
        return ref.at[pl.ds(which * HALF, HALF), :]

    project(0)
    project(1)
    pair_got(0)
    qs[0] = pair_sum(0, 0, Q).astype(BF)
    send(half(qs.at[0], 0), rla, rx_ss.at[0], rx_rs.at[0], right)
    send(half(qs.at[0], 1), rlb, rx_ss.at[1], rx_rs.at[1], left)
    project(2)
    pair_got(1)
    qs[1, HALF:Q, :] = pair_sum(1, HALF, HALF).astype(BF)
    send(half(qs.at[1], 1), half(fl, 1), rx_ss.at[2], rx_rs.at[2], right)
    pair_got(2)
    qs[2, 0:HALF, :] = pair_sum(2, 0, HALF).astype(BF)
    send(half(qs.at[2], 0), half(fr, 0), rx_ss.at[3], rx_rs.at[3], left)

    ag_got(4)
    ag_got(5)
    ag_pair_got(4)
    ag_pair_got(5)
    grad_mix_of(x_at(2))
    run_v[...] = jnp.zeros_like(run_v)

    @pl.loop(0, CHUNKS)
    def _(back):
        c = CHUNKS - 1 - back
        run = run_v[...]
        arr_v[c] = run.astype(BF)
        run_v[...] = own_v[c] + bd_v[c, 0:1, :] * run

    b1s[...] = run_v[...].astype(BF)
    b1r[y] = b1s[own_q, :]
    for r in range(1, NY):
        q_rows = pl.ds(pl.multiple_of(((y + r) % NY) * QR, QR), QR)
        send(b1s.at[q_rows, :], b1r.at[y], b1_ss.at[r], b1_rs.at[r], y_peer(r))

    project(3)

    def relay():
        remote(half(qs.at[0], 0), rla, rx_ss.at[0], rx_rs.at[0], right).wait_recv()
        qs[1, 0:HALF, :] = (pair_sum(1, 0, HALF) + rla[...].astype(F32)).astype(BF)
        send(half(qs.at[1], 0), half(fl, 0), rx_ss.at[4], rx_rs.at[4], right)
        remote(half(qs.at[0], 1), rlb, rx_ss.at[1], rx_rs.at[1], left).wait_recv()
        qs[2, HALF:Q, :] = (pair_sum(2, HALF, HALF) + rlb[...].astype(F32)).astype(BF)
        send(half(qs.at[2], 1), half(fr, 1), rx_ss.at[5], rx_rs.at[5], left)

    def grad_chunk(c):
        rows = rows_of(c)
        b = wk[rows, :]
        for p in range(PAIRS):
            dyp = dy_v[rows, pair(p)]
            grad = dot(wt_v[c, p], doubled(dyp))
            grad += exc_v[rows, pair(p)].astype(F32) * dot(b, arr_v[c, :, pair(p)])
            gl_v[rows, pair(p)] = grad + skip_rows[p] * dyp.astype(F32)

    pl.loop(0, 4)(grad_chunk)

    for r in range(1, NY):
        source = (y + NY - r) % NY
        remote(b1s.at[own_q, :], b1r.at[source], b1_ss.at[r], b1_rs.at[r], y_peer(r)).wait_recv()
    bzs[...] = sum(
        zrow_v[NY + j : NY + j + 1, :] * b1r[j].astype(F32) for j in range(NY)
    ).astype(BF)
    bzr[z] = bzs[...]
    for r in range(1, NZ):
        send(bzs, bzr.at[z], bz_ss.at[r], bz_rs.at[r], z_peer(r))

    relay()
    pl.loop(4, CHUNKS)(grad_chunk)

    for r in range(1, NZ):
        source = (z + NZ - r) % NZ
        remote(bzs, bzr.at[source], bz_ss.at[r], bz_rs.at[r], z_peer(r)).wait_recv()
    row_state = sum(zrow_b[i : i + 1, :] * bzr[i].astype(F32) for i in range(NZ))
    for k in range(NY):
        out = brow_v[6 + k : 7 + k, :] * row_state
        for place, (kk, j) in enumerate(in_row):
            if kk == k:
                out += brow_v[place : place + 1, :] * b1r[j].astype(F32)
        b2s[k * QR : (k + 1) * QR, :] = out.astype(BF)
    b2r[own_q, :] = b2s[own_q, :]
    for r in range(1, NY):
        q_rows = pl.ds(pl.multiple_of(((y + r) % NY) * QR, QR), QR)
        send(b2s.at[q_rows, :], b2r.at[own_q, :], b2_ss.at[r], b2_rs.at[r], y_peer(r))

    pair_got(3)
    qs[3] = pair_sum(3, 0, Q).astype(BF)

    for r in range(1, NY):
        source = pl.ds(pl.multiple_of(((y + NY - r) % NY) * QR, QR), QR)
        remote(b2s.at[own_q, :], b2r.at[source, :], b2_ss.at[r], b2_rs.at[r], y_peer(r)).wait_recv()

    @pl.loop(0, CHUNKS)
    def _(c):
        rows = rows_of(c)
        carried = exs_v[rows, :].astype(F32) * dot(wk[rows, :], b2r[...])
        gi[rows, :] = (gl_v[rows, :] + carried).astype(BF)

    remote(half(qs.at[1], 1), half(fl, 1), rx_ss.at[2], rx_rs.at[2], right).wait_recv()
    remote(half(qs.at[2], 0), half(fr, 0), rx_ss.at[3], rx_rs.at[3], left).wait_recv()
    remote(half(qs.at[1], 0), half(fl, 0), rx_ss.at[4], rx_rs.at[4], right).wait_recv()
    remote(half(qs.at[2], 1), half(fr, 1), rx_ss.at[5], rx_rs.at[5], left).wait_recv()
    mo[...] = (qs[3].astype(F32) + fl[...].astype(F32) + fr[...].astype(F32)).astype(BF)

    for copy in started:
        copy.wait_send()


def shards(
    inputs, gates, write_keys, read_keys, log_decay, skip_gain, doc_ids, out_weight, grad_out
):
    vmem = pl.BlockSpec(memory_space=pltpu.VMEM)
    smem = pl.BlockSpec(memory_space=pltpu.SMEM)
    hbm = pl.BlockSpec(memory_space=pl.ANY)
    v = lambda shape, kind=BF: pltpu.VMEM(shape, kind)
    dma = lambda *shape: pltpu.SemaphoreType.DMA(shape)
    full = (TOK, WIDTH)
    scratch = [
        v(full), v(full), v((WIDTH, D)), v((TOK, D)), v(full, F32), v(full, F32), v(full, F32),
        v(full), v(full), v(full), v(full), v((CHUNKS, PAIRS, Q, 2 * Q)), v(full),
        v((CHUNKS, N, WIDTH)), v((CHUNKS, N, WIDTH)), v((CHUNKS, N, WIDTH), F32),
        v((N, WIDTH), F32), v((128, TOK), F32), v((TOK, 128), F32), v((CHUNKS, 16, Q), F32),
        v((TOK, 128), F32), v((CHUNKS, 8, WIDTH), F32), v((8, 128), F32), v((8, 128), F32),
        v((128, WIDTH)),
        v((N, WIDTH)), v((NY, QR, WIDTH)), v((8, 128), F32), v((NY, 8, 128), F32),
        v((QR, WIDTH)), v((NZ, QR, WIDTH)), v((8, 128), F32), v((NZ, 8, 128), F32),
        v((N, WIDTH)), v((N, WIDTH)), v((16, WIDTH), F32), v((16, WIDTH), F32),
        v((8, WIDTH), F32),
        v((N, WIDTH)), v((NY, QR, WIDTH)), v((QR, WIDTH)), v((NZ, QR, WIDTH)),
        v((N, WIDTH)), v((N, WIDTH)),
        v((NX, 2 * Q, D)), v((NX, Q, D)), v((NX, Q, D)), v((HALF, D)), v((HALF, D)),
        v((Q, D)), v((Q, D)),
        dma(4), dma(6), dma(6), dma(7), dma(7),
        dma(NY), dma(NY), dma(NY), dma(NY), dma(NZ), dma(NZ), dma(NZ), dma(NZ), dma(NY), dma(NY),
        dma(NY), dma(NY), dma(NZ), dma(NZ), dma(NY), dma(NY),
        dma(4), dma(4), dma(6), dma(6),
    ]
    return pl.pallas_call(
        kernel,
        out_shape=(
            jax.ShapeDtypeStruct((Q, D), BF),
            jax.ShapeDtypeStruct((TOK, WIDTH), BF),
        ),
        in_specs=[hbm, hbm, vmem, vmem, vmem, smem, vmem, hbm, hbm],
        out_specs=(vmem, vmem),
        scratch_shapes=scratch,
        compiler_params=pltpu.CompilerParams(
            collective_id=0, has_side_effects=True, vmem_limit_bytes=60 * 1024 * 1024
        ),
    )(
        inputs, gates, write_keys, read_keys, log_decay, skip_gain,
        doc_ids.reshape(CHUNKS, Q), out_weight, grad_out,
    )


def solution(mesh):
    return jax.shard_map(
        shards,
        mesh=mesh,
        in_specs=(
            P("seq", "head"),
            P("seq", "head"),
            P("seq", None),
            P("seq", None),
            P("head", "seq"),
            P("head"),
            P("seq"),
            P("head", None),
            P(("seq", "head"), None),
        ),
        out_specs=(P(("seq", "head"), None), P("seq", "head")),
        check_vma=False,
    )
```

time: 248 us -> 71.7 us (0.29)
  waiting for transfers between devices: 72 us -> 0 us
  Pallas kernels: 0 us -> 66.7 us
  blocking collectives: 60.5 us -> 0 us
  local copies, waits for them, and re-layouts: 39.4 us -> 3.13 us
  matrix products: 30.2 us -> 0 us
  other arithmetic: 22.3 us -> 0 us
  between operations: 15.8 us -> 0.65 us
  starting transfers between devices: 5.11 us -> 0 us
    pallas_call x0 -> x1, Pallas kernels: none -> 66.7 us  [shards(): pl.pallas_call(kernel, out_shape=(jax.ShapeDtypeStruct((Q, D), BF), jax.S...]
    all_gather x5 -> x0, blocking collectives: 60.5 us -> none  [entering_2(): lax.all_gather(part.astype(kind), axis)]
    all_gather x4 -> x0, waiting for transfers between devices: 38.7 us -> none  [the longest x2 22.5 us: gather_in_order(): pieces = lax.all_gather(pieces, axes[k], axis=0, tiled=True)]
    reduce_scatter x1 -> x0, waiting for transfers between devices: 31.8 us -> none  [shards(): lax.psum_scatter(jnp.dot(gated, out_weight, preferred_element_type=jnp.fl...]
    dot_general x9 -> x0, matrix products: 30.2 us -> none  [the longest x1 8.79 us: shards(): jnp.dot(gated, out_weight, preferred_element_type=jnp.float32)]
    reshape x6 -> x0, local copies, waits for them, and re-layouts: 11.8 us -> none  [the longest x1 3.85 us: shards(): blocks_x = inputs.reshape(group_count, GROUP, head_count, head_width)]
    another operation x7 -> x0, other arithmetic: 11.1 us -> none
    unnamed x92 -> x4, local copies, waits for them, and re-layouts: 11.3 us -> 3.13 us
  transfers between devices with their start and end apart: 6 -> 0, of which waited for: 3 -> 0; matrix products, arithmetic and copies ran while one was open for 29% -> 0% of each run, Pallas kernels for 0% -> 0%
where the time goes in v1:
time: 71.7 us; the launch traced here: 70.5 us
  Pallas kernels  66.7 us (93%)
  local copies, waits for them, and re-layouts  3.13 us (4%)
    pallas_call x1, Pallas kernels, shards(): pl.pallas_call(kernel, out_shape=(jax.ShapeDtypeStruct((Q, D), BF), jax.S...  66.7 us
    unnamed x4, local copies, waits for them, and re-layouts  3.13 us

profile of v1, /device:TPU:1, one launch (start us, length us, event | category | flops | bytes accessed | tf_op | source)
XLA Modules:
  0.0 70.5 jit_solution(3962275884695946881)
XLA Ops:
  0.6 66.7 %shard_map.104 = (bf16[128,2560]{1,0:T(8,128)(2,1)}, bf16[1024,640]{1,0:T(8,128)(2,1)}) custom-call(bf16[1024,640]{1,0:T(8,128)(2,1)} %x_hbm.1, bf16[1024,640]{1,0:T(8,128)(2,1)} %g_hbm.1, bf16[1024,128]{1,0:T(8,128)(2,1)} %wk.1, bf16[1024,128]{1,0:T(8,128)(2,1)} %rk.1, f32[10,1024]{1,0:T(8,128)} %ld.1, f32[10]{0:T(128)} %skip.1, s32[8,128]{1,0:T(8,128)} %bitcast.1, ...), custom_call_target="tpu_custom_call" | custom-call | tf_op jit(solution)/shard_map/pallas_call | solution.py:514
  67.4 0.0 copy-start
  67.4 2.1 %copy.13 = bf16[128,2560]{1,0:T(8,128)(2,1)} copy(bf16[128,2560]{1,0:T(8,128)(2,1)} %get-tuple-element.4) | data formatting | bytes 1310720
  69.5 0.0 copy-done
  69.5 1.1 %copy.14 = bf16[1024,640]{1,0:T(8,128)(2,1)} copy(bf16[1024,640]{1,0:T(8,128)(2,1)S(1)} %copy-done) | data formatting | bytes 2621440
Async XLA Ops:
  67.4 2.1 %copy-start = (bf16[1024,640]{1,0:T(8,128)(2,1)S(1)}, bf16[1024,640]{1,0:T(8,128)(2,1)}, u32[]{:S(2)}) copy-start(bf16[1024,640]{1,0:T(8,128)(2,1)} %get-tuple-element.5) | copy-start | bytes 3932164

commit v2 on v1

--- a/solution.py
+++ b/solution.py
@@ -53,10 +53,11 @@
 
 
 def kernel(
-    x_hbm, g_hbm, wk, rk, ld, skip, docs, wo_hbm, go_hbm,
+    x_hbm, g_hbm, wk_hbm, rk_hbm, ld, skip, docs, wo_hbm, go_hbm,
     mo, gi,
-    x_v, g_v, wo_v, go_v, silu_v, mix_v, gl_v, exc_v, enc_v, exs_v, ens_v, wt_v, dy_v,
-    enter_v, arr_v, own_v, run_v, ldp_v, ccol_v, crow_v, dt_v, bd_v, off_v, prev_v, spread_v,
+    x_v, g_v, wk, rk, wo_v, go_v, silu_v, mix_v, gl_v, exc_v, enc_v, exs_v, ens_v, wt_v, dy_v,
+    enter_v, arr_v, own_v, run_v, ldp_v, docm_v, ccol_v, crow_v, wexc_v, wenc_v, wens_v, bd_v,
+    spread_v,
     y1s, y1r, m1s, m1r, zs, zr, mzs, mzr, y2s, y2r, wrow_v, brow_v, zrow_v,
     b1s, b1r, bzs, bzr, b2s, b2r,
     pall, pr, qs, rla, rlb, fl, fr,
@@ -94,34 +95,75 @@
 
     own_rows = pl.ds(pl.multiple_of(head * Q, Q), Q)
     loads = [
-        pltpu.make_async_copy(go_hbm, go_v.at[own_rows, :], lsem.at[0]),
-        pltpu.make_async_copy(x_hbm, x_v, lsem.at[1]),
-        pltpu.make_async_copy(g_hbm, g_v, lsem.at[2]),
-        pltpu.make_async_copy(wo_hbm, wo_v, lsem.at[3]),
+        pltpu.make_async_copy(x_hbm, x_v, lsem.at[0]),
+        pltpu.make_async_copy(wk_hbm, wk, lsem.at[1]),
+        pltpu.make_async_copy(rk_hbm, rk, lsem.at[2]),
+        pltpu.make_async_copy(g_hbm, g_v, lsem.at[3]),
+        pltpu.make_async_copy(go_hbm, go_v.at[own_rows, :], lsem.at[4]),
+        pltpu.make_async_copy(wo_hbm, wo_v, lsem.at[5]),
     ]
-    for copy in loads:
-        copy.start()
 
     barrier = pltpu.get_barrier_semaphore()
     peers = [right, left, partner]
     peers += [y_peer(r) for r in range(1, NY)] + [z_peer(r) for r in range(1, NZ)]
     for peer in peers:
         pl.semaphore_signal(barrier, inc=1, device_id=peer, device_id_type=MESH)
+    for copy in loads:
+        copy.start()
+
+    sub = lax.broadcasted_iota(jnp.int32, (Q, Q), 0)
+    lane = lax.broadcasted_iota(jnp.int32, (Q, Q), 1)
+    ones = lambda condition: condition.astype(F32).astype(BF)
+    tri = ones(lane <= sub)
+    eye = ones(lane == sub)
+    head_lane = lax.broadcasted_iota(jnp.int32, (1, 128), 1)
+    same_head = (sub % 16) == (lane % 16)
+    head_of = lax.broadcasted_iota(jnp.int32, (128, WIDTH), 1) // HP
+    spread_v[...] = ones(head_of == lax.broadcasted_iota(jnp.int32, (128, WIDTH), 0) % 16)
+    m_lo = ones(head_lane < HP)
+    m_hi = ones(head_lane >= HP)
+
+    def in_block(c):
+        return ones(head_lane // 16 == c)
+
+    def expand_row(w):
+        w = jnp.where(head_lane < 16, w, 0.0)
+        a = w.astype(BF)
+        return dot(a, spread_v[...]) + dot((w - a.astype(F32)).astype(BF), spread_v[...])
+
+    def rows_of(c):
+        return pl.ds(pl.multiple_of(c * Q, Q), Q)
+
+    ldp_v[...] = jnp.zeros_like(ldp_v)
+    for c in range(CHUNKS):
+        ldp_v[16 * c : 16 * c + HEADS, :] = ld[:, c * Q : (c + 1) * Q] * LOG2E
+        docm_v[16 * c : 16 * c + 16, :] = jnp.broadcast_to(docs[c : c + 1, :].astype(F32), (16, Q))
+    parts = split3(ldp_v[...])
+    ccol_all = sum(dot_nt(tri, part) for part in parts)
+    ccol_v[...] = ccol_all
+    dt_all = dot_nt(eye, docm_v[...].astype(BF))
+    c_end, d_end = ccol_all[Q - 1 : Q, :], dt_all[Q - 1 : Q, :]
+    df = jnp.broadcast_to(docm_v[0:1, 0:1], (1, 128))
+    dl = jnp.broadcast_to(docm_v[127:128, 127:128], (1, 128))
+    end_parts = split3(jnp.broadcast_to(c_end, (8, 128)))
+    before = ones(same_head & (sub // 16 < lane // 16))
+    off = sum(dot(part, before) for part in end_parts)[0:1, :]
+    total = sum(dot(part, ones(same_head)) for part in end_parts)[0:1, :]
+    prev = jnp.where(head_lane < 16, df, pltpu.roll(d_end, 16, 1))
+    w_exs = jnp.where(dt_all == dl, jnp.exp2(total - off - ccol_all), 0.0).astype(BF)
+
     pl.semaphore_wait(barrier, len(peers))
 
     def go_rows(place, of_core, half):
         start = pl.multiple_of((place * 2 + of_core) * Q + half * HALF, HALF)
         return go_v.at[pl.ds(start, HALF), :]
 
-    loads[0].wait()
     for half in (0, 1):
-        ref = go_rows(xx, core, half)
-        send(ref, ref, agx_s.at[half], agx_r.at[half], right)
-    for half in (1, 0):
-        ref = go_rows(xx, core, half)
-        send(ref, ref, agx_s.at[2 + half], agx_r.at[2 + half], left)
-    own_ref = go_v.at[own_rows, :]
-    send(own_ref, own_ref, agd_s.at[6], agd_r.at[6], partner)
+        part = go_hbm.at[pl.ds(half * HALF, HALF), :]
+        send(part, go_rows(xx, core, half), agx_s.at[half], agx_r.at[half], right)
+        part = go_hbm.at[pl.ds((1 - half) * HALF, HALF), :]
+        send(part, go_rows(xx, core, 1 - half), agx_s.at[3 - half], agx_r.at[3 - half], left)
+    send(go_hbm, go_v.at[own_rows, :], agd_s.at[6], agd_r.at[6], partner)
 
     def ag_got(unit):
         place = x_at((3, 3, 1, 1, 2, 2)[unit])
@@ -138,68 +180,14 @@
         ref = go_rows(place, 1 - core, unit % 2)
         remote(ref, ref, agd_s.at[unit], agd_r.at[unit], partner).wait_recv()
 
-    sub = lax.broadcasted_iota(jnp.int32, (Q, Q), 0)
-    lane = lax.broadcasted_iota(jnp.int32, (Q, Q), 1)
-    tri = (lane <= sub).astype(F32).astype(BF)
-    eye = (lane == sub).astype(F32).astype(BF)
-    head_lane = lax.broadcasted_iota(jnp.int32, (1, 128), 1)
-    lane_row = (lax.broadcasted_iota(jnp.int32, (128, WIDTH), 1) // HP)
-    head_row = lax.broadcasted_iota(jnp.int32, (128, WIDTH), 0)
-    spread_v[...] = (lane_row == head_row).astype(F32).astype(BF)
-    m_lo = (head_lane < HP).astype(F32).astype(BF)
-    m_hi = (head_lane >= HP).astype(F32).astype(BF)
-
-    def expand(w):
-        return dot(w.astype(BF), spread_v[...])
-
-    def expand_fine(w):
-        a = w.astype(BF)
-        return dot(a, spread_v[...]) + dot((w - a.astype(F32)).astype(BF), spread_v[...])
-
-    def rows_of(c):
-        return pl.ds(pl.multiple_of(c * Q, Q), Q)
-
-    ldp_v[...] = jnp.zeros_like(ldp_v)
-    ldp_v[0:HEADS, :] = ld[...] * LOG2E
-    doc_f = docs[...].astype(F32)
-    df = jnp.broadcast_to(doc_f[0:1, 0:1], (1, 128))
-    off_v[...] = jnp.zeros_like(off_v)
-    prev_v[...] = jnp.broadcast_to(df, prev_v.shape)
-    run_v[...] = jnp.zeros_like(run_v)
+    loads[0].wait()
+    for c in range(CHUNKS):
+        rows = slice(c * Q, (c + 1) * Q)
+        exs = dot(w_exs * in_block(c), spread_v[...]).astype(BF)
+        exs_v[rows, :] = exs
+        dy_v[rows, :] = x_v[rows, :] * exs
     loads[1].wait()
-
-    @pl.loop(0, CHUNKS)
-    def _(c):
-        rows = rows_of(c)
-        cols = rows_of(c)
-        parts = split3(ldp_v[:, cols])
-        ccol = sum(dot_nt(tri, part) for part in parts)
-        ccol_v[rows, :] = ccol
-        crow_v[c] = sum(dot_nt(part[0:16], tri) for part in parts)
-        doc_row = docs[pl.ds(c, 1), :].astype(F32)
-        dt = dot_nt(eye, jnp.broadcast_to(doc_row, (Q, Q)).astype(BF))
-        dt_v[rows, :] = dt
-        c_end, d_end = ccol[Q - 1 : Q, :], dt[Q - 1 : Q, :]
-        exc = expand(jnp.where(dt == d_end, jnp.exp2(c_end - ccol), 0.0)).astype(BF)
-        exc_v[rows, :] = exc
-        prev = prev_v[0:1, :]
-        bd = jnp.where(d_end == prev, jnp.exp2(c_end), 0.0)
-        bdx = expand_fine(jnp.broadcast_to(bd, (8, 128)))
-        bd_v[c] = bdx
-        own = dot_tn(wk[rows, :], x_v[rows, :] * exc)
-        run = run_v[...]
-        enter_v[c] = run.astype(BF)
-        run_v[...] = run * bdx[0:1, :] + own
-        entw = jnp.where(dt == prev, jnp.exp2(ccol), 0.0)
-        enc_v[rows, :] = expand(entw).astype(BF)
-        off = off_v[0:1, :]
-        ens_v[rows, :] = expand(jnp.where(dt == df, jnp.exp2(ccol + off), 0.0)).astype(BF)
-        prev_v[...] = jnp.broadcast_to(d_end, prev_v.shape)
-        off_v[...] = jnp.broadcast_to(off + c_end, off_v.shape)
-
-    total = off_v[0:1, :]
-    dl = prev_v[0:1, :]
-    y1s[...] = run_v[...].astype(BF)
+    y1s[...] = dot_tn(wk[...], dy_v[...]).astype(BF)
     m1s[...] = stacked([total, df, dl], 8)
     own_q = pl.ds(pl.multiple_of(y * QR, QR), QR)
     m1r[y] = m1s[...]
@@ -219,18 +207,39 @@
     def doubled(v):
         return jnp.concatenate([v * m_lo, v * m_hi], axis=0)
 
+    crow_v[...] = sum(dot_nt(part, tri) for part in parts)
+    wexc_v[...] = jnp.where(dt_all == d_end, jnp.exp2(c_end - ccol_all), 0.0).astype(BF)
+    wenc_v[...] = jnp.where(dt_all == prev, jnp.exp2(ccol_all), 0.0).astype(BF)
+    wens_v[...] = jnp.where(dt_all == df, jnp.exp2(ccol_all + off), 0.0).astype(BF)
+    block_decay = jnp.where(d_end == prev, jnp.exp2(c_end), 0.0)
+    of_block = lax.broadcasted_iota(jnp.int32, (CHUNKS, 128), 0) == (
+        lax.broadcasted_iota(jnp.int32, (CHUNKS, 128), 1) // 16
+    )
+    block_decay = jnp.where(of_block, block_decay, 0.0)
+    coarse = block_decay.astype(BF)
+    fine = (block_decay - coarse.astype(F32)).astype(BF)
+    bd_v[...] = dot(coarse, spread_v[...]) + dot(fine, spread_v[...])
+    run_v[...] = jnp.zeros_like(run_v)
+
     def inner_chunk(c):
         rows = rows_of(c)
-        ccol, dt = ccol_v[rows, :], dt_v[rows, :]
-        crow = crow_v[c]
-        same = dt == docs[pl.ds(c, 1), :].astype(F32)
+        mine_only = in_block(c)
+        exc = dot(wexc_v[...] * mine_only, spread_v[...]).astype(BF)
+        exc_v[rows, :] = exc
+        enc = dot(wenc_v[...] * mine_only, spread_v[...])
+        enc_v[rows, :] = enc.astype(BF)
+        ens_v[rows, :] = dot(wens_v[...] * mine_only, spread_v[...]).astype(BF)
+        run = run_v[...]
+        enter_v[c] = run.astype(BF)
         b, k = wk[rows, :], rk[rows, :]
+        run_v[...] = run * bd_v[pl.ds(c, 1), :] + dot_tn(b, x_v[rows, :] * exc)
+        ccol = pltpu.roll(ccol_v[...], (128 - 16 * c) % 128, 1)
+        crow = crow_v[pl.ds(pl.multiple_of(c * 16, 16), 16), :]
+        doc_row = docs[pl.ds(c, 1), :].astype(F32)
+        dt = dot_nt(eye, jnp.broadcast_to(doc_row, (Q, Q)).astype(BF))
+        same = dt == doc_row
         sm = jnp.where(same & (sub >= lane), dot_nt(k, b), 0.0)
         stm = jnp.where(same & (lane >= sub), dot_nt(b, k), 0.0)
-        off_c = off_v[0:1, :]
-        shard_c = ccol + off_c
-        exs = jnp.where(dt == dl, jnp.exp2(total - shard_c), 0.0)
-        exs_v[rows, :] = expand(exs).astype(BF)
         for p in range(PAIRS):
             ws, wts = [], []
             for h in (2 * p, 2 * p + 1):
@@ -244,10 +253,9 @@
             mix_v[rows, pair(p)] = mixed + skip_rows[p] * xp.astype(F32)
             gate = g_v[rows, pair(p)].astype(F32)
             silu_v[rows, pair(p)] = gate / (1.0 + jnp.exp(-gate))
-        off_v[...] = jnp.broadcast_to(off_c + ccol[Q - 1 : Q, :], off_v.shape)
-
-    off_v[...] = jnp.zeros_like(off_v)
+
     loads[2].wait()
+    loads[3].wait()
     pl.loop(0, 4)(inner_chunk)
 
     for r in range(1, NY):
@@ -270,7 +278,7 @@
 
     t_rows = [gated_decay(dls[j], dls[NY - 1], ls[j + 1 :]) for j in range(NY)]
     t_rows += [gated_decay(dfs[j], dfs[0], ls[:j]) for j in range(NY)]
-    zrow_v[...] = expand_fine(stacked(t_rows, 8))
+    zrow_v[...] = expand_row(stacked(t_rows, 8))
     zs[...] = sum(zrow_v[j : j + 1, :] * y1r[j].astype(F32) for j in range(NY)).astype(BF)
     mzs[...] = stacked([span(ls), dfs[0], dls[NY - 1]], 8)
     zr[z] = zs[...]
@@ -282,17 +290,18 @@
     in_row = [(j, k) for k in range(NY) for j in range(k)]
     f_rows = [gated_decay(dls[j], dfs[k], ls[j + 1 : k]) for j, k in in_row]
     f_rows += [gated_decay(dfs[0], dfs[k], ls[:k]) for k in range(NY)]
-    wrow_v[...] = expand_fine(stacked(f_rows, 16))
+    wrow_v[...] = expand_row(stacked(f_rows, 16))
     b_rows = [gated_decay(dfs[k], dls[j], ls[j + 1 : k]) for j, k in in_row]
     b_rows += [gated_decay(dls[NY - 1], dls[k], ls[k + 1 :]) for k in range(NY)]
-    brow_v[...] = expand_fine(stacked(b_rows, 16))
+    brow_v[...] = expand_row(stacked(b_rows, 16))
 
     ag_got(0)
     ag_got(3)
 
     pl.loop(4, CHUNKS)(inner_chunk)
 
-    loads[3].wait()
+    loads[4].wait()
+    loads[5].wait()
 
     def grad_mix_of(place):
         rows = pl.ds(pl.multiple_of(place * 2 * Q, 2 * Q), 2 * Q)
@@ -309,6 +318,9 @@
 
     ag_got(1)
     ag_got(2)
+    ag_pair_got(0)
+    ag_pair_got(1)
+    grad_mix_of(x_at(3))
 
     for r in range(1, NZ):
         source = (z + NZ - r) % NZ
@@ -328,7 +340,7 @@
         zf_rows.append(flag(i < z) * jnp.where(rdls[i] == dfs[0], jnp.exp2(gap), 0.0))
         gap = span([rls[m] * flag(m > z) for m in range(i)])
         zb_rows.append(flag(i > z) * jnp.where(rdfs[i] == dls[NY - 1], jnp.exp2(gap), 0.0))
-    zf = expand_fine(stacked(zf_rows, 8))
+    zf = expand_row(stacked(zf_rows, 8))
     row_state = sum(zf[i : i + 1, :] * zr[i].astype(F32) for i in range(NZ))
     for k in range(NY):
         out = wrow_v[6 + k : 7 + k, :] * row_state
@@ -340,14 +352,13 @@
     for r in range(1, NY):
         q_rows = pl.ds(pl.multiple_of(((y + r) % NY) * QR, QR), QR)
         send(y2s.at[q_rows, :], y2r.at[own_q, :], y2_ss.at[r], y2_rs.at[r], y_peer(r))
-    zrow_b = expand_fine(stacked(zb_rows, 8))
-
-    ag_pair_got(0)
-    ag_pair_got(1)
-    grad_mix_of(x_at(3))
+    zrow_b = expand_row(stacked(zb_rows, 8))
+
     ag_pair_got(2)
     ag_pair_got(3)
     grad_mix_of(x_at(1))
+    ag_got(4)
+    ag_got(5)
 
     for r in range(1, NY):
         source = pl.ds(pl.multiple_of(((y + NY - r) % NY) * QR, QR), QR)
@@ -382,16 +393,7 @@
     qs[0] = pair_sum(0, 0, Q).astype(BF)
     send(half(qs.at[0], 0), rla, rx_ss.at[0], rx_rs.at[0], right)
     send(half(qs.at[0], 1), rlb, rx_ss.at[1], rx_rs.at[1], left)
-    project(2)
-    pair_got(1)
-    qs[1, HALF:Q, :] = pair_sum(1, HALF, HALF).astype(BF)
-    send(half(qs.at[1], 1), half(fl, 1), rx_ss.at[2], rx_rs.at[2], right)
-    pair_got(2)
-    qs[2, 0:HALF, :] = pair_sum(2, 0, HALF).astype(BF)
-    send(half(qs.at[2], 0), half(fr, 0), rx_ss.at[3], rx_rs.at[3], left)
-
-    ag_got(4)
-    ag_got(5)
+
     ag_pair_got(4)
     ag_pair_got(5)
     grad_mix_of(x_at(2))
@@ -402,7 +404,7 @@
         c = CHUNKS - 1 - back
         run = run_v[...]
         arr_v[c] = run.astype(BF)
-        run_v[...] = own_v[c] + bd_v[c, 0:1, :] * run
+        run_v[...] = own_v[c] + bd_v[pl.ds(c, 1), :] * run
 
     b1s[...] = run_v[...].astype(BF)
     b1r[y] = b1s[own_q, :]
@@ -410,7 +412,14 @@
         q_rows = pl.ds(pl.multiple_of(((y + r) % NY) * QR, QR), QR)
         send(b1s.at[q_rows, :], b1r.at[y], b1_ss.at[r], b1_rs.at[r], y_peer(r))
 
+    pair_got(1)
+    qs[1, HALF:Q, :] = pair_sum(1, HALF, HALF).astype(BF)
+    send(half(qs.at[1], 1), half(fl, 1), rx_ss.at[2], rx_rs.at[2], right)
+    project(2)
     project(3)
+    pair_got(2)
+    qs[2, 0:HALF, :] = pair_sum(2, 0, HALF).astype(BF)
+    send(half(qs.at[2], 0), half(fr, 0), rx_ss.at[3], rx_rs.at[3], left)
 
     def relay():
         remote(half(qs.at[0], 0), rla, rx_ss.at[0], rx_rs.at[0], right).wait_recv()
@@ -482,6 +491,17 @@
         copy.wait_send()
 
 
+def write_out(mo, gi, mo_out, gi_out, sem):
+    copies = [
+        pltpu.make_async_copy(mo, mo_out, sem.at[0]),
+        pltpu.make_async_copy(gi, gi_out, sem.at[1]),
+    ]
+    for copy in copies:
+        copy.start()
+    for copy in copies:
+        copy.wait()
+
+
 def shards(
     inputs, gates, write_keys, read_keys, log_decay, skip_gain, doc_ids, out_weight, grad_out
 ):
@@ -490,13 +510,14 @@
     hbm = pl.BlockSpec(memory_space=pl.ANY)
     v = lambda shape, kind=BF: pltpu.VMEM(shape, kind)
     dma = lambda *shape: pltpu.SemaphoreType.DMA(shape)
-    full = (TOK, WIDTH)
+    full, square = (TOK, WIDTH), (128, 128)
     scratch = [
-        v(full), v(full), v((WIDTH, D)), v((TOK, D)), v(full, F32), v(full, F32), v(full, F32),
+        v(full), v(full), v((TOK, N)), v((TOK, N)), v((WIDTH, D)), v((TOK, D)),
+        v(full, F32), v(full, F32), v(full, F32),
         v(full), v(full), v(full), v(full), v((CHUNKS, PAIRS, Q, 2 * Q)), v(full),
         v((CHUNKS, N, WIDTH)), v((CHUNKS, N, WIDTH)), v((CHUNKS, N, WIDTH), F32),
-        v((N, WIDTH), F32), v((128, TOK), F32), v((TOK, 128), F32), v((CHUNKS, 16, Q), F32),
-        v((TOK, 128), F32), v((CHUNKS, 8, WIDTH), F32), v((8, 128), F32), v((8, 128), F32),
+        v((N, WIDTH), F32), v(square, F32), v(square, F32), v(square, F32), v(square, F32),
+        v(square), v(square), v(square), v((CHUNKS, WIDTH), F32),
         v((128, WIDTH)),
         v((N, WIDTH)), v((NY, QR, WIDTH)), v((8, 128), F32), v((NY, 8, 128), F32),
         v((QR, WIDTH)), v((NZ, QR, WIDTH)), v((8, 128), F32), v((NZ, 8, 128), F32),
@@ -506,27 +527,35 @@
         v((N, WIDTH)), v((N, WIDTH)),
         v((NX, 2 * Q, D)), v((NX, Q, D)), v((NX, Q, D)), v((HALF, D)), v((HALF, D)),
         v((Q, D)), v((Q, D)),
-        dma(4), dma(6), dma(6), dma(7), dma(7),
+        dma(6), dma(6), dma(6), dma(7), dma(7),
         dma(NY), dma(NY), dma(NY), dma(NY), dma(NZ), dma(NZ), dma(NZ), dma(NZ), dma(NY), dma(NY),
         dma(NY), dma(NY), dma(NZ), dma(NZ), dma(NY), dma(NY),
         dma(4), dma(4), dma(6), dma(6),
     ]
-    return pl.pallas_call(
+    results = pl.pallas_call(
         kernel,
-        out_shape=(
-            jax.ShapeDtypeStruct((Q, D), BF),
-            jax.ShapeDtypeStruct((TOK, WIDTH), BF),
-        ),
-        in_specs=[hbm, hbm, vmem, vmem, vmem, smem, vmem, hbm, hbm],
+        out_shape=(pltpu.VMEM((Q, D), BF), pltpu.VMEM((TOK, WIDTH), BF)),
+        in_specs=[hbm, hbm, hbm, hbm, vmem, smem, vmem, hbm, hbm],
         out_specs=(vmem, vmem),
         scratch_shapes=scratch,
         compiler_params=pltpu.CompilerParams(
-            collective_id=0, has_side_effects=True, vmem_limit_bytes=60 * 1024 * 1024
+            collective_id=0, has_side_effects=True, vmem_limit_bytes=54 * 1024 * 1024
         ),
     )(
         inputs, gates, write_keys, read_keys, log_decay, skip_gain,
         doc_ids.reshape(CHUNKS, Q), out_weight, grad_out,
     )
+    return pl.pallas_call(
+        write_out,
+        out_shape=(
+            jax.ShapeDtypeStruct((Q, D), BF),
+            jax.ShapeDtypeStruct((TOK, WIDTH), BF),
+        ),
+        in_specs=[vmem, vmem],
+        out_specs=(hbm, hbm),
+        scratch_shapes=[dma(2)],
+        compiler_params=pltpu.CompilerParams(vmem_limit_bytes=1024 * 1024),
+    )(*results)
 
 
 def solution(mesh):

time: 71.7 us -> 65.6 us (0.915); the launches traced: 70.5 us -> 65.5 us
  local copies, waits for them, and re-layouts: 3.13 us -> 0 us
  Pallas kernels: 66.7 us -> 64.9 us
    unnamed x4 -> x0, local copies, waits for them, and re-layouts: 3.13 us -> none
    pallas_call x1 -> x2, Pallas kernels: 66.7 us -> 64.9 us  [the longest x1 63.6 us: shards(): pl.pallas_call(kernel, out_shape=(pltpu.VMEM((Q, D), BF), pltpu.VMEM((TOK...]
where the time goes in v2:
time: 65.6 us; the launch traced here: 65.5 us
  Pallas kernels  64.9 us (99%)
    pallas_call x1, Pallas kernels, shards(): pl.pallas_call(kernel, out_shape=(pltpu.VMEM((Q, D), BF), pltpu.VMEM((TOK...  63.6 us

profile of v2, /device:TPU:1, one launch (start us, length us, event | category | flops | bytes accessed | tf_op | source)
XLA Modules:
  0.0 65.5 jit_solution(2741761885404798641)
XLA Ops:
  0.6 63.6 %shard_map.104 = (bf16[128,2560]{1,0:T(8,128)(2,1)S(1)}, bf16[1024,640]{1,0:T(8,128)(2,1)S(1)}) custom-call(bf16[1024,640]{1,0:T(8,128)(2,1)} %x_hbm.1, bf16[1024,640]{1,0:T(8,128)(2,1)} %g_hbm.1, bf16[1024,128]{1,0:T(8,128)(2,1)} %wk_hbm.1, bf16[1024,128]{1,0:T(8,128)(2,1)} %rk_hbm.1, f32[10,1024]{1,0:T(8,128)} %ld.1, f32[10]{0:T(128)} %skip.1, ...), custom_call_target="tpu_custom_call" | custom-call | tf_op jit(solution)/shard_map/pallas_call | solution.py:535
  64.2 1.3 %shard_map.105 = (bf16[128,2560]{1,0:T(8,128)(2,1)}, bf16[1024,640]{1,0:T(8,128)(2,1)}) custom-call(bf16[128,2560]{1,0:T(8,128)(2,1)S(1)} %get-tuple-element.4.mo, bf16[1024,640]{1,0:T(8,128)(2,1)S(1)} %get-tuple-element.5.gi), custom_call_target="tpu_custom_call" | custom-call | tf_op jit(solution)/shard_map/pallas_call | solution.py:548

commit v3 on v2

--- a/solution.py
+++ b/solution.py
@@ -56,7 +56,7 @@
     x_hbm, g_hbm, wk_hbm, rk_hbm, ld, skip, docs, wo_hbm, go_hbm,
     mo, gi,
     x_v, g_v, wk, rk, wo_v, go_v, silu_v, mix_v, gl_v, exc_v, enc_v, exs_v, ens_v, wt_v, dy_v,
-    enter_v, arr_v, own_v, run_v, ldp_v, docm_v, ccol_v, crow_v, wexc_v, wenc_v, wens_v, bd_v,
+    enter_v, arr_v, gsum_v, run_v, ldp_v, docm_v, ccol_v, crow_v, wexc_v, wenc_v, wens_v, bd_v,
     spread_v,
     y1s, y1r, m1s, m1r, zs, zr, mzs, mzr, y2s, y2r, wrow_v, brow_v, zrow_v,
     b1s, b1r, bzs, bzr, b2s, b2r,
@@ -110,6 +110,18 @@
         pl.semaphore_signal(barrier, inc=1, device_id=peer, device_id_type=MESH)
     for copy in loads:
         copy.start()
+    pl.semaphore_wait(barrier, len(peers))
+
+    def go_rows(place, of_core, half):
+        start = pl.multiple_of((place * 2 + of_core) * Q + half * HALF, HALF)
+        return go_v.at[pl.ds(start, HALF), :]
+
+    for half in (0, 1):
+        part = go_hbm.at[pl.ds(half * HALF, HALF), :]
+        send(part, go_rows(xx, core, half), agx_s.at[half], agx_r.at[half], right)
+        part = go_hbm.at[pl.ds((1 - half) * HALF, HALF), :]
+        send(part, go_rows(xx, core, 1 - half), agx_s.at[3 - half], agx_r.at[3 - half], left)
+    send(go_hbm, go_v.at[own_rows, :], agd_s.at[6], agd_r.at[6], partner)
 
     sub = lax.broadcasted_iota(jnp.int32, (Q, Q), 0)
     lane = lax.broadcasted_iota(jnp.int32, (Q, Q), 1)
@@ -151,19 +163,6 @@
     total = sum(dot(part, ones(same_head)) for part in end_parts)[0:1, :]
     prev = jnp.where(head_lane < 16, df, pltpu.roll(d_end, 16, 1))
     w_exs = jnp.where(dt_all == dl, jnp.exp2(total - off - ccol_all), 0.0).astype(BF)
-
-    pl.semaphore_wait(barrier, len(peers))
-
-    def go_rows(place, of_core, half):
-        start = pl.multiple_of((place * 2 + of_core) * Q + half * HALF, HALF)
-        return go_v.at[pl.ds(start, HALF), :]
-
-    for half in (0, 1):
-        part = go_hbm.at[pl.ds(half * HALF, HALF), :]
-        send(part, go_rows(xx, core, half), agx_s.at[half], agx_r.at[half], right)
-        part = go_hbm.at[pl.ds((1 - half) * HALF, HALF), :]
-        send(part, go_rows(xx, core, 1 - half), agx_s.at[3 - half], agx_r.at[3 - half], left)
-    send(go_hbm, go_v.at[own_rows, :], agd_s.at[6], agd_r.at[6], partner)
 
     def ag_got(unit):
         place = x_at((3, 3, 1, 1, 2, 2)[unit])
@@ -303,18 +302,17 @@
     loads[4].wait()
     loads[5].wait()
 
-    def grad_mix_of(place):
+    def grad_mix_of(place, first=False):
         rows = pl.ds(pl.multiple_of(place * 2 * Q, 2 * Q), 2 * Q)
         grad = dot_nt(go_v[rows, :], wo_v[...])
-        dy_v[rows, :] = (grad * silu_v[rows, :]).astype(BF)
-        for k in (0, 1):
-            c = place * 2 + k
-            one = rows_of(c)
-            own_v[c] = dot_tn(rk[one, :], dy_v[one, :] * enc_v[one, :])
+        dy = (grad * silu_v[rows, :]).astype(BF)
+        dy_v[rows, :] = dy
+        state = dot_tn(rk[rows, :], dy * ens_v[rows, :])
+        gsum_v[...] = state if first else gsum_v[...] + state
 
     pair_own = go_v.at[pl.ds(pl.multiple_of((xx * 2 + 1 - core) * Q, Q), Q), :]
     remote(pair_own, pair_own, agd_s.at[6], agd_r.at[6], partner).wait_recv()
-    grad_mix_of(xx)
+    grad_mix_of(xx, first=True)
 
     ag_got(1)
     ag_got(2)
@@ -357,8 +355,6 @@
     ag_pair_got(2)
     ag_pair_got(3)
     grad_mix_of(x_at(1))
-    ag_got(4)
-    ag_got(5)
 
     for r in range(1, NY):
         source = pl.ds(pl.multiple_of(((y + NY - r) % NY) * QR, QR), QR)
@@ -394,19 +390,12 @@
     send(half(qs.at[0], 0), rla, rx_ss.at[0], rx_rs.at[0], right)
     send(half(qs.at[0], 1), rlb, rx_ss.at[1], rx_rs.at[1], left)
 
+    ag_got(4)
+    ag_got(5)
     ag_pair_got(4)
     ag_pair_got(5)
     grad_mix_of(x_at(2))
-    run_v[...] = jnp.zeros_like(run_v)
-
-    @pl.loop(0, CHUNKS)
-    def _(back):
-        c = CHUNKS - 1 - back
-        run = run_v[...]
-        arr_v[c] = run.astype(BF)
-        run_v[...] = own_v[c] + bd_v[pl.ds(c, 1), :] * run
-
-    b1s[...] = run_v[...].astype(BF)
+    b1s[...] = gsum_v[...].astype(BF)
     b1r[y] = b1s[own_q, :]
     for r in range(1, NY):
         q_rows = pl.ds(pl.multiple_of(((y + r) % NY) * QR, QR), QR)
@@ -429,13 +418,20 @@
         qs[2, HALF:Q, :] = (pair_sum(2, HALF, HALF) + rlb[...].astype(F32)).astype(BF)
         send(half(qs.at[2], 1), half(fr, 1), rx_ss.at[5], rx_rs.at[5], left)
 
-    def grad_chunk(c):
+    run_v[...] = jnp.zeros_like(run_v)
+
+    def grad_chunk(back):
+        c = CHUNKS - 1 - back
         rows = rows_of(c)
         b = wk[rows, :]
+        run = run_v[...]
+        run_v[...] = bd_v[pl.ds(c, 1), :] * run + dot_tn(rk[rows, :], dy_v[rows, :] * enc_v[rows, :])
+        arr = run.astype(BF)
+        arr_v[...] = arr
         for p in range(PAIRS):
             dyp = dy_v[rows, pair(p)]
             grad = dot(wt_v[c, p], doubled(dyp))
-            grad += exc_v[rows, pair(p)].astype(F32) * dot(b, arr_v[c, :, pair(p)])
+            grad += exc_v[rows, pair(p)].astype(F32) * dot(b, arr_v[:, pair(p)])
             gl_v[rows, pair(p)] = grad + skip_rows[p] * dyp.astype(F32)
 
     pl.loop(0, 4)(grad_chunk)
@@ -475,9 +471,9 @@
         source = pl.ds(pl.multiple_of(((y + NY - r) % NY) * QR, QR), QR)
         remote(b2s.at[own_q, :], b2r.at[source, :], b2_ss.at[r], b2_rs.at[r], y_peer(r)).wait_recv()
 
-    @pl.loop(0, CHUNKS)
-    def _(c):
-        rows = rows_of(c)
+    @pl.loop(0, CHUNKS // 2)
+    def _(k):
+        rows = pl.ds(pl.multiple_of(k * 2 * Q, 2 * Q), 2 * Q)
         carried = exs_v[rows, :].astype(F32) * dot(wk[rows, :], b2r[...])
         gi[rows, :] = (gl_v[rows, :] + carried).astype(BF)
 
@@ -515,7 +511,7 @@
         v(full), v(full), v((TOK, N)), v((TOK, N)), v((WIDTH, D)), v((TOK, D)),
         v(full, F32), v(full, F32), v(full, F32),
         v(full), v(full), v(full), v(full), v((CHUNKS, PAIRS, Q, 2 * Q)), v(full),
-        v((CHUNKS, N, WIDTH)), v((CHUNKS, N, WIDTH)), v((CHUNKS, N, WIDTH), F32),
+        v((CHUNKS, N, WIDTH)), v((N, WIDTH)), v((N, WIDTH), F32),
         v((N, WIDTH), F32), v(square, F32), v(square, F32), v(square, F32), v(square, F32),
         v(square), v(square), v(square), v((CHUNKS, WIDTH), F32),
         v((128, WIDTH)),

time: 65.6 us -> 65.4 us (level)
  no operation moved by 1% of the time
where the time goes in v3:
time: 65.4 us; the launch traced here: 65.3 us
  Pallas kernels  64.7 us (99%)
    pallas_call x1, Pallas kernels, shards(): pl.pallas_call(kernel, out_shape=(pltpu.VMEM((Q, D), BF), pltpu.VMEM((TOK...  63.4 us

profile of v3, /device:TPU:1, one launch (start us, length us, event | category | flops | bytes accessed | tf_op | source)
XLA Modules:
  0.0 65.3 jit_solution(8770915111377549483)
XLA Ops:
  0.6 63.4 %shard_map.104 = (bf16[128,2560]{1,0:T(8,128)(2,1)S(1)}, bf16[1024,640]{1,0:T(8,128)(2,1)S(1)}) custom-call(bf16[1024,640]{1,0:T(8,128)(2,1)} %x_hbm.1, bf16[1024,640]{1,0:T(8,128)(2,1)} %g_hbm.1, bf16[1024,128]{1,0:T(8,128)(2,1)} %wk_hbm.1, bf16[1024,128]{1,0:T(8,128)(2,1)} %rk_hbm.1, f32[10,1024]{1,0:T(8,128)} %ld.1, f32[10]{0:T(128)} %skip.1, ...), custom_call_target="tpu_custom_call" | custom-call | tf_op jit(solution)/shard_map/pallas_call | solution.py:531
  64.0 1.3 %shard_map.105 = (bf16[128,2560]{1,0:T(8,128)(2,1)}, bf16[1024,640]{1,0:T(8,128)(2,1)}) custom-call(bf16[128,2560]{1,0:T(8,128)(2,1)S(1)} %get-tuple-element.4.mo, bf16[1024,640]{1,0:T(8,128)(2,1)S(1)} %get-tuple-element.5.gi), custom_call_target="tpu_custom_call" | custom-call | tf_op jit(solution)/shard_map/pallas_call | solution.py:544

commit v4 on v3

--- a/solution.py
+++ b/solution.py
@@ -8,6 +8,7 @@
 from jax.sharding import PartitionSpec as P
 
 NX, NY, NZ = 4, 4, 8
+Y_STEPS, Z_STEPS = (2, 1, 3), (4, 3, 5, 2, 6, 1, 7)
 Q = 128
 CHUNKS = 8
 TOK = Q * CHUNKS
@@ -58,7 +59,7 @@
     x_v, g_v, wk, rk, wo_v, go_v, silu_v, mix_v, gl_v, exc_v, enc_v, exs_v, ens_v, wt_v, dy_v,
     enter_v, arr_v, gsum_v, run_v, ldp_v, docm_v, ccol_v, crow_v, wexc_v, wenc_v, wens_v, bd_v,
     spread_v,
-    y1s, y1r, m1s, m1r, zs, zr, mzs, mzr, y2s, y2r, wrow_v, brow_v, zrow_v,
+    y1s, y1r, m1s, m1r, zs, zr, mzs, mzr, y2s, y2r, wrow_v, brow_v, zrow_v, zf_v, zb_v,
     b1s, b1r, bzs, bzr, b2s, b2r,
     pall, pr, qs, rla, rlb, fl, fr,
     lsem, agx_s, agx_r, agd_s, agd_r,
@@ -105,7 +106,7 @@
 
     barrier = pltpu.get_barrier_semaphore()
     peers = [right, left, partner]
-    peers += [y_peer(r) for r in range(1, NY)] + [z_peer(r) for r in range(1, NZ)]
+    peers += [y_peer(r) for r in Y_STEPS] + [z_peer(r) for r in Z_STEPS]
     for peer in peers:
         pl.semaphore_signal(barrier, inc=1, device_id=peer, device_id_type=MESH)
     for copy in loads:
@@ -179,6 +180,11 @@
         ref = go_rows(place, 1 - core, unit % 2)
         remote(ref, ref, agd_s.at[unit], agd_r.at[unit], partner).wait_recv()
 
+    m1s[...] = stacked([total, df, dl], 8)
+    m1r[y] = m1s[...]
+    for r in Y_STEPS:
+        send(m1s, m1r.at[y], m1_ss.at[r], m1_rs.at[r], y_peer(r))
+
     loads[0].wait()
     for c in range(CHUNKS):
         rows = slice(c * Q, (c + 1) * Q)
@@ -187,13 +193,10 @@
         dy_v[rows, :] = x_v[rows, :] * exs
     loads[1].wait()
     y1s[...] = dot_tn(wk[...], dy_v[...]).astype(BF)
-    m1s[...] = stacked([total, df, dl], 8)
     own_q = pl.ds(pl.multiple_of(y * QR, QR), QR)
-    m1r[y] = m1s[...]
     y1r[y] = y1s[own_q, :]
-    for r in range(1, NY):
+    for r in Y_STEPS:
         q_rows = pl.ds(pl.multiple_of(((y + r) % NY) * QR, QR), QR)
-        send(m1s, m1r.at[y], m1_ss.at[r], m1_rs.at[r], y_peer(r))
         send(y1s.at[q_rows, :], y1r.at[y], y1_ss.at[r], y1_rs.at[r], y_peer(r))
 
     skip_rows = [
@@ -255,12 +258,11 @@
 
     loads[2].wait()
     loads[3].wait()
-    pl.loop(0, 4)(inner_chunk)
-
-    for r in range(1, NY):
+    pl.loop(0, 2)(inner_chunk)
+
+    for r in Y_STEPS:
         source = (y + NY - r) % NY
         remote(m1s, m1r.at[source], m1_ss.at[r], m1_rs.at[r], y_peer(r)).wait_recv()
-        remote(y1s.at[own_q, :], y1r.at[source], y1_ss.at[r], y1_rs.at[r], y_peer(r)).wait_recv()
     meta = [m1r[j] for j in range(NY)]
     ls = [m[0:1, :] for m in meta]
     dfs = [m[1:2, :] for m in meta]
@@ -275,17 +277,13 @@
     def gated_decay(a, b, values):
         return jnp.where(a == b, jnp.exp2(span(values)), 0.0)
 
+    mzs[...] = stacked([span(ls), dfs[0], dls[NY - 1]], 8)
+    mzr[z] = mzs[...]
+    for r in Z_STEPS:
+        send(mzs, mzr.at[z], mz_ss.at[r], mz_rs.at[r], z_peer(r))
     t_rows = [gated_decay(dls[j], dls[NY - 1], ls[j + 1 :]) for j in range(NY)]
     t_rows += [gated_decay(dfs[j], dfs[0], ls[:j]) for j in range(NY)]
     zrow_v[...] = expand_row(stacked(t_rows, 8))
-    zs[...] = sum(zrow_v[j : j + 1, :] * y1r[j].astype(F32) for j in range(NY)).astype(BF)
-    mzs[...] = stacked([span(ls), dfs[0], dls[NY - 1]], 8)
-    zr[z] = zs[...]
-    mzr[z] = mzs[...]
-    for r in range(1, NZ):
-        send(mzs, mzr.at[z], mz_ss.at[r], mz_rs.at[r], z_peer(r))
-        send(zs, zr.at[z], z_ss.at[r], z_rs.at[r], z_peer(r))
-
     in_row = [(j, k) for k in range(NY) for j in range(k)]
     f_rows = [gated_decay(dls[j], dfs[k], ls[j + 1 : k]) for j, k in in_row]
     f_rows += [gated_decay(dfs[0], dfs[k], ls[:k]) for k in range(NY)]
@@ -294,6 +292,16 @@
     b_rows += [gated_decay(dls[NY - 1], dls[k], ls[k + 1 :]) for k in range(NY)]
     brow_v[...] = expand_row(stacked(b_rows, 16))
 
+    pl.loop(2, 4)(inner_chunk)
+
+    for r in Y_STEPS:
+        source = (y + NY - r) % NY
+        remote(y1s.at[own_q, :], y1r.at[source], y1_ss.at[r], y1_rs.at[r], y_peer(r)).wait_recv()
+    zs[...] = sum(zrow_v[j : j + 1, :] * y1r[j].astype(F32) for j in range(NY)).astype(BF)
+    zr[z] = zs[...]
+    for r in Z_STEPS:
+        send(zs, zr.at[z], z_ss.at[r], z_rs.at[r], z_peer(r))
+
     ag_got(0)
     ag_got(3)
 
@@ -314,16 +322,9 @@
     remote(pair_own, pair_own, agd_s.at[6], agd_r.at[6], partner).wait_recv()
     grad_mix_of(xx, first=True)
 
-    ag_got(1)
-    ag_got(2)
-    ag_pair_got(0)
-    ag_pair_got(1)
-    grad_mix_of(x_at(3))
-
-    for r in range(1, NZ):
+    for r in Z_STEPS:
         source = (z + NZ - r) % NZ
         remote(mzs, mzr.at[source], mz_ss.at[r], mz_rs.at[r], z_peer(r)).wait_recv()
-        remote(zs, zr.at[source], z_ss.at[r], z_rs.at[r], z_peer(r)).wait_recv()
     zmeta = [mzr[i] for i in range(NZ)]
     rls = [m[0:1, :] for m in zmeta]
     rdfs = [m[1:2, :] for m in zmeta]
@@ -338,8 +339,16 @@
         zf_rows.append(flag(i < z) * jnp.where(rdls[i] == dfs[0], jnp.exp2(gap), 0.0))
         gap = span([rls[m] * flag(m > z) for m in range(i)])
         zb_rows.append(flag(i > z) * jnp.where(rdfs[i] == dls[NY - 1], jnp.exp2(gap), 0.0))
-    zf = expand_row(stacked(zf_rows, 8))
-    row_state = sum(zf[i : i + 1, :] * zr[i].astype(F32) for i in range(NZ))
+    zf_v[...] = expand_row(stacked(zf_rows, 8))
+    zb_v[...] = expand_row(stacked(zb_rows, 8))
+
+    ag_got(1)
+    ag_got(2)
+
+    for r in Z_STEPS:
+        source = (z + NZ - r) % NZ
+        remote(zs, zr.at[source], z_ss.at[r], z_rs.at[r], z_peer(r)).wait_recv()
+    row_state = sum(zf_v[i : i + 1, :] * zr[i].astype(F32) for i in range(NZ))
     for k in range(NY):
         out = wrow_v[6 + k : 7 + k, :] * row_state
         for place, (j, kk) in enumerate(in_row):
@@ -347,16 +356,18 @@
                 out += wrow_v[place : place + 1, :] * y1r[j].astype(F32)
         y2s[k * QR : (k + 1) * QR, :] = out.astype(BF)
     y2r[own_q, :] = y2s[own_q, :]
-    for r in range(1, NY):
+    for r in Y_STEPS:
         q_rows = pl.ds(pl.multiple_of(((y + r) % NY) * QR, QR), QR)
         send(y2s.at[q_rows, :], y2r.at[own_q, :], y2_ss.at[r], y2_rs.at[r], y_peer(r))
-    zrow_b = expand_row(stacked(zb_rows, 8))
-
+
+    ag_pair_got(0)
+    ag_pair_got(1)
+    grad_mix_of(x_at(3))
     ag_pair_got(2)
     ag_pair_got(3)
     grad_mix_of(x_at(1))
 
-    for r in range(1, NY):
+    for r in Y_STEPS:
         source = pl.ds(pl.multiple_of(((y + NY - r) % NY) * QR, QR), QR)
         remote(y2s.at[own_q, :], y2r.at[source, :], y2_ss.at[r], y2_rs.at[r], y_peer(r)).wait_recv()
 
@@ -364,14 +375,21 @@
     mine = pl.ds(pl.multiple_of(core * Q, Q), Q)
     theirs = pl.ds(pl.multiple_of((1 - core) * Q, Q), Q)
 
-    def project(k):
-        rows = pl.ds(pl.multiple_of(order[k] * 2 * Q, 2 * Q), 2 * Q)
+    def project_rows(k, start, count):
+        rows = pl.ds(pl.multiple_of(order[k] * 2 * Q + start, Q), count)
+        to_rows = pl.ds(pl.multiple_of(start, Q), count)
         carried = ens_v[rows, :].astype(F32) * dot(rk[rows, :], y2r[...])
         gated = ((mix_v[rows, :] + carried) * silu_v[rows, :]).astype(BF)
         for n in range(5):
             cols = slice(n * 512, (n + 1) * 512)
-            pall[k, :, cols] = dot(gated, wo_v[:, cols]).astype(BF)
+            pall[k, to_rows, cols] = dot(gated, wo_v[:, cols]).astype(BF)
+
+    def to_partner(k):
         send(pall.at[k, theirs, :], pr.at[k], d_ss.at[k], d_rs.at[k], partner)
+
+    def project(k):
+        project_rows(k, 0, 2 * Q)
+        to_partner(k)
 
     def pair_sum(k, start, count):
         rows = pl.ds(pl.multiple_of(core * Q + start, HALF), count)
@@ -383,21 +401,23 @@
     def half(ref, which):
         return ref.at[pl.ds(which * HALF, HALF), :]
 
-    project(0)
-    project(1)
+    project_rows(0, (1 - core) * Q, Q)
+    to_partner(0)
+    project_rows(0, core * Q, Q)
+    ag_got(4)
+    ag_got(5)
     pair_got(0)
     qs[0] = pair_sum(0, 0, Q).astype(BF)
     send(half(qs.at[0], 0), rla, rx_ss.at[0], rx_rs.at[0], right)
     send(half(qs.at[0], 1), rlb, rx_ss.at[1], rx_rs.at[1], left)
-
-    ag_got(4)
-    ag_got(5)
+    project(1)
+
     ag_pair_got(4)
     ag_pair_got(5)
     grad_mix_of(x_at(2))
     b1s[...] = gsum_v[...].astype(BF)
     b1r[y] = b1s[own_q, :]
-    for r in range(1, NY):
+    for r in Y_STEPS:
         q_rows = pl.ds(pl.multiple_of(((y + r) % NY) * QR, QR), QR)
         send(b1s.at[q_rows, :], b1r.at[y], b1_ss.at[r], b1_rs.at[r], y_peer(r))
 
@@ -436,23 +456,23 @@
 
     pl.loop(0, 4)(grad_chunk)
 
-    for r in range(1, NY):
+    for r in Y_STEPS:
         source = (y + NY - r) % NY
         remote(b1s.at[own_q, :], b1r.at[source], b1_ss.at[r], b1_rs.at[r], y_peer(r)).wait_recv()
     bzs[...] = sum(
         zrow_v[NY + j : NY + j + 1, :] * b1r[j].astype(F32) for j in range(NY)
     ).astype(BF)
     bzr[z] = bzs[...]
-    for r in range(1, NZ):
+    for r in Z_STEPS:
         send(bzs, bzr.at[z], bz_ss.at[r], bz_rs.at[r], z_peer(r))
 
     relay()
     pl.loop(4, CHUNKS)(grad_chunk)
 
-    for r in range(1, NZ):
+    for r in Z_STEPS:
         source = (z + NZ - r) % NZ
         remote(bzs, bzr.at[source], bz_ss.at[r], bz_rs.at[r], z_peer(r)).wait_recv()
-    row_state = sum(zrow_b[i : i + 1, :] * bzr[i].astype(F32) for i in range(NZ))
+    row_state = sum(zb_v[i : i + 1, :] * bzr[i].astype(F32) for i in range(NZ))
     for k in range(NY):
         out = brow_v[6 + k : 7 + k, :] * row_state
         for place, (kk, j) in enumerate(in_row):
@@ -460,14 +480,14 @@
                 out += brow_v[place : place + 1, :] * b1r[j].astype(F32)
         b2s[k * QR : (k + 1) * QR, :] = out.astype(BF)
     b2r[own_q, :] = b2s[own_q, :]
-    for r in range(1, NY):
+    for r in Y_STEPS:
         q_rows = pl.ds(pl.multiple_of(((y + r) % NY) * QR, QR), QR)
         send(b2s.at[q_rows, :], b2r.at[own_q, :], b2_ss.at[r], b2_rs.at[r], y_peer(r))
 
     pair_got(3)
     qs[3] = pair_sum(3, 0, Q).astype(BF)
 
-    for r in range(1, NY):
+    for r in Y_STEPS:
         source = pl.ds(pl.multiple_of(((y + NY - r) % NY) * QR, QR), QR)
         remote(b2s.at[own_q, :], b2r.at[source, :], b2_ss.at[r], b2_rs.at[r], y_peer(r)).wait_recv()
 
@@ -518,7 +538,7 @@
         v((N, WIDTH)), v((NY, QR, WIDTH)), v((8, 128), F32), v((NY, 8, 128), F32),
         v((QR, WIDTH)), v((NZ, QR, WIDTH)), v((8, 128), F32), v((NZ, 8, 128), F32),
         v((N, WIDTH)), v((N, WIDTH)), v((16, WIDTH), F32), v((16, WIDTH), F32),
-        v((8, WIDTH), F32),
+        v((8, WIDTH), F32), v((8, WIDTH), F32), v((8, WIDTH), F32),
         v((N, WIDTH)), v((NY, QR, WIDTH)), v((QR, WIDTH)), v((NZ, QR, WIDTH)),
         v((N, WIDTH)), v((N, WIDTH)),
         v((NX, 2 * Q, D)), v((NX, Q, D)), v((NX, Q, D)), v((HALF, D)), v((HALF, D)),

time: 65.4 us -> 62.3 us (0.953)
  Pallas kernels: 64.7 us -> 61.5 us
    pallas_call x1, Pallas kernels: 63.4 us -> 60.2 us  [shards(): pl.pallas_call(kernel, out_shape=(pltpu.VMEM((Q, D), BF), pltpu.VMEM((TOK...]
where the time goes in v4:
time: 62.3 us; the launch traced here: 62.2 us
  Pallas kernels  61.5 us (99%)
  between operations  0.64 us (1%)
    pallas_call x1, Pallas kernels, shards(): pl.pallas_call(kernel, out_shape=(pltpu.VMEM((Q, D), BF), pltpu.VMEM((TOK...  60.2 us
    pallas_call x1, Pallas kernels, shards(): pl.pallas_call(write_out, out_shape=(jax.ShapeDtypeStruct((Q, D), BF), ja...  1.29 us

profile of v4, /device:TPU:1, one launch (start us, length us, event | category | flops | bytes accessed | tf_op | source)
XLA Modules:
  0.0 62.2 jit_solution(2859623136158727046)
XLA Ops:
  0.6 60.2 %shard_map.104 = (bf16[128,2560]{1,0:T(8,128)(2,1)S(1)}, bf16[1024,640]{1,0:T(8,128)(2,1)S(1)}) custom-call(bf16[1024,640]{1,0:T(8,128)(2,1)} %x_hbm.1, bf16[1024,640]{1,0:T(8,128)(2,1)} %g_hbm.1, bf16[1024,128]{1,0:T(8,128)(2,1)} %wk_hbm.1, bf16[1024,128]{1,0:T(8,128)(2,1)} %rk_hbm.1, f32[10,1024]{1,0:T(8,128)} %ld.1, f32[10]{0:T(128)} %skip.1, ...), custom_call_target="tpu_custom_call" | custom-call | tf_op jit(solution)/shard_map/pallas_call | solution.py:551
  60.9 1.3 %shard_map.105 = (bf16[128,2560]{1,0:T(8,128)(2,1)}, bf16[1024,640]{1,0:T(8,128)(2,1)}) custom-call(bf16[128,2560]{1,0:T(8,128)(2,1)S(1)} %get-tuple-element.4.mo, bf16[1024,640]{1,0:T(8,128)(2,1)S(1)} %get-tuple-element.5.gi), custom_call_target="tpu_custom_call" | custom-call | tf_op jit(solution)/shard_map/pallas_call | solution.py:564

commit v5 on v4

--- a/solution.py
+++ b/solution.py
@@ -94,6 +94,13 @@
         copy.start()
         started.append(copy)
 
+    sent_where = []
+
+    def send_where(condition, *args):
+        copy = remote(*args)
+        pl.when(condition)(copy.start)
+        sent_where.append((condition, copy))
+
     own_rows = pl.ds(pl.multiple_of(head * Q, Q), Q)
     loads = [
         pltpu.make_async_copy(x_hbm, x_v, lsem.at[0]),
@@ -104,6 +111,8 @@
         pltpu.make_async_copy(wo_hbm, wo_v, lsem.at[5]),
     ]
 
+    zr[...] = jnp.zeros_like(zr)
+    bzr[...] = jnp.zeros_like(bzr)
     barrier = pltpu.get_barrier_semaphore()
     peers = [right, left, partner]
     peers += [y_peer(r) for r in Y_STEPS] + [z_peer(r) for r in Z_STEPS]
@@ -122,7 +131,7 @@
         send(part, go_rows(xx, core, half), agx_s.at[half], agx_r.at[half], right)
         part = go_hbm.at[pl.ds((1 - half) * HALF, HALF), :]
         send(part, go_rows(xx, core, 1 - half), agx_s.at[3 - half], agx_r.at[3 - half], left)
-    send(go_hbm, go_v.at[own_rows, :], agd_s.at[6], agd_r.at[6], partner)
+    send(go_hbm, go_v.at[own_rows, :], agd_s.at[8], agd_r.at[8], partner)
 
     sub = lax.broadcasted_iota(jnp.int32, (Q, Q), 0)
     lane = lax.broadcasted_iota(jnp.int32, (Q, Q), 1)
@@ -165,19 +174,26 @@
     prev = jnp.where(head_lane < 16, df, pltpu.roll(d_end, 16, 1))
     w_exs = jnp.where(dt_all == dl, jnp.exp2(total - off - ccol_all), 0.0).astype(BF)
 
+    def ag_rows(unit, of_core):
+        if unit < 4:
+            return go_rows(x_at((3, 3, 1, 1)[unit]), of_core, unit % 2)
+        start = (x_at(2) * 2 + of_core) * Q + (unit - 4) * (HALF // 2)
+        return go_v.at[pl.ds(pl.multiple_of(start, HALF // 2), HALF // 2), :]
+
     def ag_got(unit):
-        place = x_at((3, 3, 1, 1, 2, 2)[unit])
-        ref = go_rows(place, core, unit % 2)
+        ref = ag_rows(unit, core)
         remote(ref, ref, agx_s.at[unit], agx_r.at[unit], left).wait_recv()
-        if unit == 0:
-            send(ref, ref, agx_s.at[4], agx_r.at[4], right)
-        if unit == 3:
-            send(ref, ref, agx_s.at[5], agx_r.at[5], left)
+        if unit in (0, 3):
+            place, to = (x_at(3), right) if unit == 0 else (x_at(1), left)
+            for piece in (0, 1):
+                start = (place * 2 + core) * Q + (unit % 2) * HALF + piece * (HALF // 2)
+                rows = pl.ds(pl.multiple_of(start, HALF // 2), HALF // 2)
+                far = 4 + (unit % 2) * 2 + piece
+                send(go_v.at[rows, :], go_v.at[rows, :], agx_s.at[far], agx_r.at[far], to)
         send(ref, ref, agd_s.at[unit], agd_r.at[unit], partner)
 
     def ag_pair_got(unit):
-        place = x_at((3, 3, 1, 1, 2, 2)[unit])
-        ref = go_rows(place, 1 - core, unit % 2)
+        ref = ag_rows(unit, 1 - core)
         remote(ref, ref, agd_s.at[unit], agd_r.at[unit], partner).wait_recv()
 
     m1s[...] = stacked([total, df, dl], 8)
@@ -300,7 +316,7 @@
     zs[...] = sum(zrow_v[j : j + 1, :] * y1r[j].astype(F32) for j in range(NY)).astype(BF)
     zr[z] = zs[...]
     for r in Z_STEPS:
-        send(zs, zr.at[z], z_ss.at[r], z_rs.at[r], z_peer(r))
+        send_where(z + r < NZ, zs, zr.at[z], z_ss.at[r], z_rs.at[r], z_peer(r))
 
     ag_got(0)
     ag_got(3)
@@ -310,16 +326,19 @@
     loads[4].wait()
     loads[5].wait()
 
-    def grad_mix_of(place, first=False):
-        rows = pl.ds(pl.multiple_of(place * 2 * Q, 2 * Q), 2 * Q)
+    def grad_mix_rows(start, count, first=False):
+        rows = pl.ds(pl.multiple_of(start, Q), count)
         grad = dot_nt(go_v[rows, :], wo_v[...])
         dy = (grad * silu_v[rows, :]).astype(BF)
         dy_v[rows, :] = dy
         state = dot_tn(rk[rows, :], dy * ens_v[rows, :])
         gsum_v[...] = state if first else gsum_v[...] + state
 
+    def grad_mix_of(place, first=False):
+        grad_mix_rows(place * 2 * Q, 2 * Q, first)
+
     pair_own = go_v.at[pl.ds(pl.multiple_of((xx * 2 + 1 - core) * Q, Q), Q), :]
-    remote(pair_own, pair_own, agd_s.at[6], agd_r.at[6], partner).wait_recv()
+    remote(pair_own, pair_own, agd_s.at[8], agd_r.at[8], partner).wait_recv()
     grad_mix_of(xx, first=True)
 
     for r in Z_STEPS:
@@ -347,7 +366,8 @@
 
     for r in Z_STEPS:
         source = (z + NZ - r) % NZ
-        remote(zs, zr.at[source], z_ss.at[r], z_rs.at[r], z_peer(r)).wait_recv()
+        total_of = remote(zs, zr.at[source], z_ss.at[r], z_rs.at[r], z_peer(r))
+        pl.when(z >= r)(total_of.wait_recv)
     row_state = sum(zf_v[i : i + 1, :] * zr[i].astype(F32) for i in range(NZ))
     for k in range(NY):
         out = wrow_v[6 + k : 7 + k, :] * row_state
@@ -372,8 +392,6 @@
         remote(y2s.at[own_q, :], y2r.at[source, :], y2_ss.at[r], y2_rs.at[r], y_peer(r)).wait_recv()
 
     order = [x_at(2), x_at(1), x_at(3), xx]
-    mine = pl.ds(pl.multiple_of(core * Q, Q), Q)
-    theirs = pl.ds(pl.multiple_of((1 - core) * Q, Q), Q)
 
     def project_rows(k, start, count):
         rows = pl.ds(pl.multiple_of(order[k] * 2 * Q + start, Q), count)
@@ -384,57 +402,68 @@
             cols = slice(n * 512, (n + 1) * 512)
             pall[k, to_rows, cols] = dot(gated, wo_v[:, cols]).astype(BF)
 
-    def to_partner(k):
-        send(pall.at[k, theirs, :], pr.at[k], d_ss.at[k], d_rs.at[k], partner)
-
-    def project(k):
+    def pair_copy(k, half, of_core):
+        rows = pl.ds(pl.multiple_of(of_core * Q + half * HALF, HALF), HALF)
+        to_rows = pl.ds(half * HALF, HALF)
+        place = 2 * k + half
+        return pall.at[k, rows, :], pr.at[k, to_rows, :], d_ss.at[place], d_rs.at[place], partner
+
+    def to_partner(k, halves):
+        for half in halves:
+            send(*pair_copy(k, half, 1 - core))
+
+    def project(k, halves):
         project_rows(k, 0, 2 * Q)
-        to_partner(k)
+        to_partner(k, halves)
 
     def pair_sum(k, start, count):
         rows = pl.ds(pl.multiple_of(core * Q + start, HALF), count)
         return pall[k, rows, :].astype(F32) + pr[k, start : start + count, :].astype(F32)
 
-    def pair_got(k):
-        remote(pall.at[k, mine, :], pr.at[k], d_ss.at[k], d_rs.at[k], partner).wait_recv()
+    def pair_got(k, half):
+        remote(*pair_copy(k, half, core)).wait_recv()
 
     def half(ref, which):
         return ref.at[pl.ds(which * HALF, HALF), :]
 
     project_rows(0, (1 - core) * Q, Q)
-    to_partner(0)
+    to_partner(0, (0, 1))
     project_rows(0, core * Q, Q)
-    ag_got(4)
-    ag_got(5)
-    pair_got(0)
-    qs[0] = pair_sum(0, 0, Q).astype(BF)
-    send(half(qs.at[0], 0), rla, rx_ss.at[0], rx_rs.at[0], right)
-    send(half(qs.at[0], 1), rlb, rx_ss.at[1], rx_rs.at[1], left)
-    project(1)
-
-    ag_pair_got(4)
-    ag_pair_got(5)
-    grad_mix_of(x_at(2))
+    for unit in (4, 6, 5, 7):
+        ag_got(unit)
+    for which, to, landing in ((0, right, rla), (1, left, rlb)):
+        pair_got(0, which)
+        rows = slice(which * HALF, (which + 1) * HALF)
+        qs[0, rows, :] = pair_sum(0, which * HALF, HALF).astype(BF)
+        send(half(qs.at[0], which), landing, rx_ss.at[which], rx_rs.at[which], to)
+
+    grad_mix_rows((x_at(2) * 2 + core) * Q, Q)
+    for unit in (4, 6, 5, 7):
+        ag_pair_got(unit)
+    grad_mix_rows((x_at(2) * 2 + 1 - core) * Q, Q)
     b1s[...] = gsum_v[...].astype(BF)
     b1r[y] = b1s[own_q, :]
     for r in Y_STEPS:
         q_rows = pl.ds(pl.multiple_of(((y + r) % NY) * QR, QR), QR)
         send(b1s.at[q_rows, :], b1r.at[y], b1_ss.at[r], b1_rs.at[r], y_peer(r))
 
-    pair_got(1)
+    project(1, (1, 0))
+    project(2, (0, 1))
+    pair_got(1, 1)
     qs[1, HALF:Q, :] = pair_sum(1, HALF, HALF).astype(BF)
     send(half(qs.at[1], 1), half(fl, 1), rx_ss.at[2], rx_rs.at[2], right)
-    project(2)
-    project(3)
-    pair_got(2)
+    pair_got(2, 0)
     qs[2, 0:HALF, :] = pair_sum(2, 0, HALF).astype(BF)
     send(half(qs.at[2], 0), half(fr, 0), rx_ss.at[3], rx_rs.at[3], left)
+    project(3, (0, 1))
 
     def relay():
         remote(half(qs.at[0], 0), rla, rx_ss.at[0], rx_rs.at[0], right).wait_recv()
+        pair_got(1, 0)
         qs[1, 0:HALF, :] = (pair_sum(1, 0, HALF) + rla[...].astype(F32)).astype(BF)
         send(half(qs.at[1], 0), half(fl, 0), rx_ss.at[4], rx_rs.at[4], right)
         remote(half(qs.at[0], 1), rlb, rx_ss.at[1], rx_rs.at[1], left).wait_recv()
+        pair_got(2, 1)
         qs[2, HALF:Q, :] = (pair_sum(2, HALF, HALF) + rlb[...].astype(F32)).astype(BF)
         send(half(qs.at[2], 1), half(fr, 1), rx_ss.at[5], rx_rs.at[5], left)
 
@@ -464,14 +493,15 @@
     ).astype(BF)
     bzr[z] = bzs[...]
     for r in Z_STEPS:
-        send(bzs, bzr.at[z], bz_ss.at[r], bz_rs.at[r], z_peer(r))
+        send_where(z + r >= NZ, bzs, bzr.at[z], bz_ss.at[r], bz_rs.at[r], z_peer(r))
 
     relay()
     pl.loop(4, CHUNKS)(grad_chunk)
 
     for r in Z_STEPS:
         source = (z + NZ - r) % NZ
-        remote(bzs, bzr.at[source], bz_ss.at[r], bz_rs.at[r], z_peer(r)).wait_recv()
+        total_of = remote(bzs, bzr.at[source], bz_ss.at[r], bz_rs.at[r], z_peer(r))
+        pl.when(z < r)(total_of.wait_recv)
     row_state = sum(zb_v[i : i + 1, :] * bzr[i].astype(F32) for i in range(NZ))
     for k in range(NY):
         out = brow_v[6 + k : 7 + k, :] * row_state
@@ -484,7 +514,8 @@
         q_rows = pl.ds(pl.multiple_of(((y + r) % NY) * QR, QR), QR)
         send(b2s.at[q_rows, :], b2r.at[own_q, :], b2_ss.at[r], b2_rs.at[r], y_peer(r))
 
-    pair_got(3)
+    pair_got(3, 0)
+    pair_got(3, 1)
     qs[3] = pair_sum(3, 0, Q).astype(BF)
 
     for r in Y_STEPS:
@@ -505,13 +536,18 @@
 
     for copy in started:
         copy.wait_send()
+    for condition, copy in sent_where:
+        pl.when(condition)(copy.wait_send)
 
 
 def write_out(mo, gi, mo_out, gi_out, sem):
-    copies = [
-        pltpu.make_async_copy(mo, mo_out, sem.at[0]),
-        pltpu.make_async_copy(gi, gi_out, sem.at[1]),
-    ]
+    copies = []
+    for ref, out in ((mo, mo_out), (gi, gi_out)):
+        count = ref.shape[0] // 4
+        for k in range(4):
+            rows = pl.ds(k * count, count)
+            place = sem.at[len(copies)]
+            copies.append(pltpu.make_async_copy(ref.at[rows, :], out.at[rows, :], place))
     for copy in copies:
         copy.start()
     for copy in copies:
@@ -543,10 +579,10 @@
         v((N, WIDTH)), v((N, WIDTH)),
         v((NX, 2 * Q, D)), v((NX, Q, D)), v((NX, Q, D)), v((HALF, D)), v((HALF, D)),
         v((Q, D)), v((Q, D)),
-        dma(6), dma(6), dma(6), dma(7), dma(7),
+        dma(6), dma(8), dma(8), dma(9), dma(9),
         dma(NY), dma(NY), dma(NY), dma(NY), dma(NZ), dma(NZ), dma(NZ), dma(NZ), dma(NY), dma(NY),
         dma(NY), dma(NY), dma(NZ), dma(NZ), dma(NY), dma(NY),
-        dma(4), dma(4), dma(6), dma(6),
+        dma(8), dma(8), dma(6), dma(6),
     ]
     results = pl.pallas_call(
         kernel,
@@ -569,7 +605,7 @@
         ),
         in_specs=[vmem, vmem],
         out_specs=(hbm, hbm),
-        scratch_shapes=[dma(2)],
+        scratch_shapes=[dma(8)],
         compiler_params=pltpu.CompilerParams(vmem_limit_bytes=1024 * 1024),
     )(*results)
 

time: 62.3 us -> 64.2 us (1.030)
  Pallas kernels: 61.5 us -> 63.4 us
    pallas_call x1, Pallas kernels: 60.2 us -> 62.1 us  [shards(): pl.pallas_call(kernel, out_shape=(pltpu.VMEM((Q, D), BF), pltpu.VMEM((TOK...]
where the time goes in v5:
time: 64.2 us; the launch traced here: 64.1 us
  Pallas kernels  63.4 us (99%)
    pallas_call x1, Pallas kernels, shards(): pl.pallas_call(kernel, out_shape=(pltpu.VMEM((Q, D), BF), pltpu.VMEM((TOK...  62.1 us
    pallas_call x1, Pallas kernels, shards(): pl.pallas_call(write_out, out_shape=(jax.ShapeDtypeStruct((Q, D), BF), ja...  1.34 us

profile of v5, /device:TPU:1, one launch (start us, length us, event | category | flops | bytes accessed | tf_op | source)
XLA Modules:
  0.0 64.1 jit_solution(290254323184125111)
XLA Ops:
  0.6 62.1 %shard_map.104 = (bf16[128,2560]{1,0:T(8,128)(2,1)S(1)}, bf16[1024,640]{1,0:T(8,128)(2,1)S(1)}) custom-call(bf16[1024,640]{1,0:T(8,128)(2,1)} %x_hbm.1, bf16[1024,640]{1,0:T(8,128)(2,1)} %g_hbm.1, bf16[1024,128]{1,0:T(8,128)(2,1)} %wk_hbm.1, bf16[1024,128]{1,0:T(8,128)(2,1)} %rk_hbm.1, f32[10,1024]{1,0:T(8,128)} %ld.1, f32[10]{0:T(128)} %skip.1, ...), custom_call_target="tpu_custom_call" | custom-call | tf_op jit(solution)/shard_map/pallas_call | solution.py:587
  62.7 1.3 %shard_map.105 = (bf16[128,2560]{1,0:T(8,128)(2,1)}, bf16[1024,640]{1,0:T(8,128)(2,1)}) custom-call(bf16[128,2560]{1,0:T(8,128)(2,1)S(1)} %get-tuple-element.4.mo, bf16[1024,640]{1,0:T(8,128)(2,1)S(1)} %get-tuple-element.5.gi), custom_call_target="tpu_custom_call" | custom-call | tf_op jit(solution)/shard_map/pallas_call | solution.py:600

commit v6 on v5

--- a/solution.py
+++ b/solution.py
@@ -431,31 +431,30 @@
     project_rows(0, core * Q, Q)
     for unit in (4, 6, 5, 7):
         ag_got(unit)
+    project(1, (1, 0))
     for which, to, landing in ((0, right, rla), (1, left, rlb)):
         pair_got(0, which)
         rows = slice(which * HALF, (which + 1) * HALF)
         qs[0, rows, :] = pair_sum(0, which * HALF, HALF).astype(BF)
         send(half(qs.at[0], which), landing, rx_ss.at[which], rx_rs.at[which], to)
 
-    grad_mix_rows((x_at(2) * 2 + core) * Q, Q)
     for unit in (4, 6, 5, 7):
         ag_pair_got(unit)
-    grad_mix_rows((x_at(2) * 2 + 1 - core) * Q, Q)
+    grad_mix_of(x_at(2))
     b1s[...] = gsum_v[...].astype(BF)
     b1r[y] = b1s[own_q, :]
     for r in Y_STEPS:
         q_rows = pl.ds(pl.multiple_of(((y + r) % NY) * QR, QR), QR)
         send(b1s.at[q_rows, :], b1r.at[y], b1_ss.at[r], b1_rs.at[r], y_peer(r))
 
-    project(1, (1, 0))
-    project(2, (0, 1))
     pair_got(1, 1)
     qs[1, HALF:Q, :] = pair_sum(1, HALF, HALF).astype(BF)
     send(half(qs.at[1], 1), half(fl, 1), rx_ss.at[2], rx_rs.at[2], right)
+    project(2, (0, 1))
+    project(3, (0, 1))
     pair_got(2, 0)
     qs[2, 0:HALF, :] = pair_sum(2, 0, HALF).astype(BF)
     send(half(qs.at[2], 0), half(fr, 0), rx_ss.at[3], rx_rs.at[3], left)
-    project(3, (0, 1))
 
     def relay():
         remote(half(qs.at[0], 0), rla, rx_ss.at[0], rx_rs.at[0], right).wait_recv()

time: 64.2 us -> 61.5 us (0.958)
  Pallas kernels: 63.4 us -> 60.8 us
    pallas_call x1, Pallas kernels: 62.1 us -> 59.4 us  [shards(): pl.pallas_call(kernel, out_shape=(pltpu.VMEM((Q, D), BF), pltpu.VMEM((TOK...]
where the time goes in v6:
time: 61.5 us; the launch traced here: 61.4 us
  Pallas kernels  60.8 us (99%)
  between operations  0.64 us (1%)
    pallas_call x1, Pallas kernels, shards(): pl.pallas_call(kernel, out_shape=(pltpu.VMEM((Q, D), BF), pltpu.VMEM((TOK...  59.4 us
    pallas_call x1, Pallas kernels, shards(): pl.pallas_call(write_out, out_shape=(jax.ShapeDtypeStruct((Q, D), BF), ja...  1.34 us

profile of v6, /device:TPU:1, one launch (start us, length us, event | category | flops | bytes accessed | tf_op | source)
XLA Modules:
  0.0 61.4 jit_solution(8859714334502316756)
XLA Ops:
  0.6 59.4 %shard_map.104 = (bf16[128,2560]{1,0:T(8,128)(2,1)S(1)}, bf16[1024,640]{1,0:T(8,128)(2,1)S(1)}) custom-call(bf16[1024,640]{1,0:T(8,128)(2,1)} %x_hbm.1, bf16[1024,640]{1,0:T(8,128)(2,1)} %g_hbm.1, bf16[1024,128]{1,0:T(8,128)(2,1)} %wk_hbm.1, bf16[1024,128]{1,0:T(8,128)(2,1)} %rk_hbm.1, f32[10,1024]{1,0:T(8,128)} %ld.1, f32[10]{0:T(128)} %skip.1, ...), custom_call_target="tpu_custom_call" | custom-call | tf_op jit(solution)/shard_map/pallas_call | solution.py:586
  60.1 1.3 %shard_map.105 = (bf16[128,2560]{1,0:T(8,128)(2,1)}, bf16[1024,640]{1,0:T(8,128)(2,1)}) custom-call(bf16[128,2560]{1,0:T(8,128)(2,1)S(1)} %get-tuple-element.4.mo, bf16[1024,640]{1,0:T(8,128)(2,1)S(1)} %get-tuple-element.5.gi), custom_call_target="tpu_custom_call" | custom-call | tf_op jit(solution)/shard_map/pallas_call | solution.py:599
